TPU v7x, 32 devices: a whole 2x2x4 slice. The times are simulated.
32 devices in a mesh: grp: 2 (over y), seq: 4 (over z), section: 2 (over x), head: 2 (over core).
Axes of the slice: x: 2, y: 2, z: 4, core: 2. Of those that a mesh axis runs over, the one named last changes fastest.
Arguments:
- queries: bfloat16 [2048, 2048], P(('grp', 'seq'), ('section', 'head')), parts along dimension 0, may hold values from -6 to 6
- reflect_keys: bfloat16 [2048, 2, 2048], P(('grp', 'seq'), None, ('section', 'head')), parts along dimension 0, may hold values from -6 to 6
- reflect_values: bfloat16 [2048, 2, 2048], P(('grp', 'seq'), None, ('section', 'head')), parts along dimension 0, may hold values from -6 to 6
- reflect_betas: float32 [2048, 2, 16], P(('grp', 'seq'), None, ('section', 'head')), parts along dimension 0, may hold values from 0 to 2
- decay_rates: float32 [2048, 16], P(('grp', 'seq'), ('section', 'head')), parts along dimension 0, may hold values from 0 to 1
- resets: int32 [2048], P(('grp', 'seq')), parts along dimension 0, may hold values 0 or 1
- out_weight: bfloat16 [2048, 2048], P(('section', 'head')), may hold values from -0.125 to 0.125
- out_cotangent: bfloat16 [2048, 2048], P(('grp', 'seq'), ('section', 'head')), parts along dimension 0, may hold values from -6 to 6
Outputs:
- output_features: bfloat16 [2048, 2048], P(('section', 'head'), ('grp', 'seq')), parts along dimension 1
- value_grads: float32 [2048, 2, 2048], P(('grp', 'seq'), None, ('section', 'head')), parts along dimension 0
There are 2 independent parts, one for each index of `grp`. A program takes and returns all parts, laid end to end along the dimension named above; an argument that names none is the same for every part. Nothing has to cross between parts.
Inputs may be any that keep to these rules, and one draw needn't show every extreme that they name: `resets`: 1 marks a token before which the state is cleared.
All inputs are finite; a program needn't handle non-finite values. No bound on the sum of `resets` on one device may be relied on, other than what follows from the above.
Results may differ from a plain program's by a relative error of at most 0.005.
Values may be sent and summed in bfloat16 or wider, within the bound.
A program may use at most 128 MiB of HBM per device.

v0:
```python
import functools
import jax
import jax.numpy as jnp
from jax import lax
from jax.experimental import pallas as pl
from jax.experimental.pallas import tpu as pltpu
from jax.sharding import PartitionSpec as P

HALF = 64
BLK = 2 * HALF
F32 = jnp.float32
BF16 = jnp.bfloat16
NN = (((1,), (0,)), ((), ()))
NT = (((1,), (1,)), ((), ()))
TN = (((0,), (0,)), ((), ()))


def dot1(a, b, dims=NN):
    return lax.dot_general(a.astype(BF16), b.astype(BF16), dims, preferred_element_type=F32)


def halves(a):
    high = a.astype(BF16)
    return high, (a - high.astype(F32)).astype(BF16)


def dot3(a, b, dims=NN):
    ah, al = halves(a)
    bh, bl = halves(b)
    d = functools.partial(lax.dot_general, dimension_numbers=dims, preferred_element_type=F32)
    return d(ah, bh) + (d(ah, bl) + d(al, bh))


def iota(shape, axis):
    return lax.broadcasted_iota(jnp.int32, shape, axis)


def step_token(index):
    block, rest = index // BLK, index % BLK
    return block * HALF + rest % HALF, rest // HALF


def local_kernel(rows_ref, cols_ref, q_ref, k0_ref, k1_ref, v0_ref, v1_ref,
                 y_ref, r_ref, m_ref, o_ref, b_ref):
    tokens, width = q_ref.shape
    blocks = tokens // HALF
    steps = 2 * tokens
    rows, cols = rows_ref[0], cols_ref[0]
    tok_s, ref_s = step_token(iota((tokens, steps), 1))
    source = iota((tokens, steps), 0)
    upto = (source <= tok_s).astype(F32)
    before = jnp.where(ref_s == 1, upto, (source < tok_s).astype(F32))
    high = functools.partial(lax.dot_general, precision=lax.Precision.HIGHEST,
                             preferred_element_type=F32)
    c_row = high(rows[:, :tokens], before, NN)[0:1]
    z_row = high(rows[:, :tokens], upto, NN)[1:2]
    beta_row = rows[2:3, tokens:]
    tok_c, ref_c = step_token(iota((steps, tokens), 0))
    source_c = iota((steps, tokens), 1)
    upto_c = (source_c <= tok_c).astype(F32)
    before_c = jnp.where(ref_c == 1, upto_c, (source_c < tok_c).astype(F32))
    c_col = high(before_c, cols[:tokens], NN)[:, 0:1]
    z_col = high(upto_c, cols[:tokens], NN)[:, 1:2]
    beta_col = cols[tokens:, 2:3]
    c_end, z_end = c_row[:, steps - 1:], z_row[:, steps - 1:]
    gamma_row = jnp.where(z_row == 0, jnp.exp(-c_row), 0.0)
    gamma_end_row = jnp.where(z_row == z_end, jnp.exp(c_row - c_end), 0.0)
    gamma_end = jnp.where(z_end == 0, jnp.exp(-c_end), 0.0)

    def sl(b):
        return slice(b * BLK, (b + 1) * BLK)

    keys, values = [], []
    for b in range(blocks):
        t = slice(b * HALF, (b + 1) * HALF)
        keys.append(jnp.concatenate([k0_ref[t, :], k1_ref[t, :]], axis=0))
        values.append(jnp.concatenate([v0_ref[t, :], v1_ref[t, :]], axis=0))
    eye = iota((BLK, BLK), 0) == iota((BLK, BLK), 1)
    tm_r = 2 * (iota((BLK, BLK), 0) % HALF) + iota((BLK, BLK), 0) // HALF
    tm_c = 2 * (iota((BLK, BLK), 1) % HALF) + iota((BLK, BLK), 1) // HALF

    gram = [[dot1(keys[b], keys[c], NT) for c in range(b + 1)] for b in range(blocks)]
    scale_row, scale_col = [], []
    for b in range(blocks):
        diag = jnp.where(eye, gram[b][b], 0.0)
        scale_row.append(lax.rsqrt(jnp.sum(diag, axis=0, keepdims=True) + 1e-6))
        scale_col.append(lax.rsqrt(jnp.sum(diag, axis=1, keepdims=True) + 1e-6))

    low = [[None] * blocks for _ in range(blocks)]
    for b in range(blocks):
        left = beta_col[sl(b)] * scale_col[b]
        for c in range(b + 1):
            valid = z_col[sl(b)] == z_row[:, sl(c)]
            if b == c:
                valid = valid & (tm_r > tm_c)
            gap = jnp.where(valid, c_row[:, sl(c)] - c_col[sl(b)], 0.0)
            low[b][c] = jnp.where(valid, jnp.exp(gap) * gram[b][c] * left * scale_row[c], 0.0)

    inverse = [jnp.where(eye, 1.0, 0.0) - jnp.where((tm_r >> 1) == (tm_c >> 1), low[b][b], 0.0)
               for b in range(blocks)]
    level = 2
    while (1 << level) <= BLK:
        pick = ((tm_r >> level) == (tm_c >> level)) & ((tm_r >> (level - 1)) != (tm_c >> (level - 1)))
        inner = [dot3(jnp.where(pick, low[b][b], 0.0), inverse[b]) for b in range(blocks)]
        inverse = [inverse[b] - dot3(inverse[b], inner[b]) for b in range(blocks)]
        level += 1

    solved = [None] * blocks
    for b in reversed(range(blocks)):
        parts = []
        kq_scale = scale_row[b]
        for a in range(b, blocks):
            t = slice(a * HALF, (a + 1) * HALF)
            product = dot1(q_ref[t, :], keys[b], NT)
            second = slice(a * BLK + HALF, (a + 1) * BLK)
            valid = z_col[second] == z_row[:, sl(b)]
            if a == b:
                valid = valid & (iota((HALF, BLK), 0) >= iota((HALF, BLK), 1) % HALF)
            gap = jnp.where(valid, c_row[:, sl(b)] - c_col[second], 0.0)
            parts.append(jnp.where(valid, jnp.exp(gap) * product * kq_scale, 0.0))
        parts.append(keys[b].astype(F32).T * (kq_scale * gamma_end_row[:, sl(b)]))
        x = jnp.concatenate(parts, axis=0)
        if b + 1 < blocks:
            later = []
            for c in range(b + 1, blocks):
                y = solved[c]
                later.append(jnp.concatenate([jnp.zeros(((c - b) * HALF, BLK), F32), y], axis=0))
            x = x - dot3(jnp.concatenate(later, axis=1),
                         jnp.concatenate([low[c][b] for c in range(b + 1, blocks)], axis=0))
        solved[b] = dot3(x, inverse[b])

    total = tokens + width
    plain = jnp.zeros((total, width), F32)
    moved = jnp.zeros((total, width), F32)
    for b in range(blocks):
        y = solved[b] * beta_row[:, sl(b)]
        if b:
            y = jnp.concatenate([jnp.zeros((b * HALF, BLK), F32), y], axis=0)
        y_ref[0, :, sl(b)] = y.astype(BF16)
        plain = plain + dot1(y, values[b])
        moved = moved + dot1(y * (gamma_row[:, sl(b)] * scale_row[b]), keys[b])
    o_ref[0] = plain[:tokens]
    b_ref[0] = plain[tokens:]
    gamma_tok = []
    for a in range(blocks):
        second = slice(a * BLK + HALF, (a + 1) * BLK)
        gamma_tok.append(jnp.where(z_col[second] == 0, jnp.exp(-c_col[second]), 0.0))
    gamma_tok = jnp.concatenate(gamma_tok, axis=0)
    r_ref[0] = (gamma_tok * q_ref[...].astype(F32) - moved[:tokens]).astype(BF16)
    m_ref[0] = jnp.where(iota((width, width), 0) == iota((width, width), 1), gamma_end, 0.0) - moved[tokens:]


def adjoint_kernel(cot_ref, w_ref, r_ref, up_ref, d_ref):
    up = dot1(cot_ref[...], w_ref[...], NT).astype(BF16)
    up_ref[0] = up
    d_ref[0] = dot1(r_ref[0], up, TN)


def finish_kernel(r_ref, o_ref, s_ref, y_ref, up_ref, ds_ref, mixed_ref, g0_ref, g1_ref):
    tokens, width = mixed_ref.shape
    mixed_ref[...] = (dot1(r_ref[0], s_ref[0]) + o_ref[0]).astype(BF16)
    right = jnp.concatenate([up_ref[0], ds_ref[0].astype(BF16)], axis=0)
    grad = dot1(y_ref[0], right, TN)
    for b in range(tokens // HALF):
        t = slice(b * HALF, (b + 1) * HALF)
        g0_ref[t, :] = grad[b * BLK:b * BLK + HALF]
        g1_ref[t, :] = grad[b * BLK + HALF:(b + 1) * BLK]


def step_order(array):
    tokens, _, heads = array.shape
    return array.reshape(tokens // HALF, HALF, 2, heads).transpose(3, 0, 2, 1).reshape(heads, 2 * tokens)


def per_device(queries, reflect_keys, reflect_values, reflect_betas, decay_rates, resets,
               out_weight, out_cotangent):
    tokens = queries.shape[0]
    heads = reflect_betas.shape[2]
    width = queries.shape[1] // heads
    steps = 2 * tokens
    devices = lax.axis_size("seq")

    cot = lax.all_gather(out_cotangent, ("section", "head"), axis=1, tiled=True)

    resets_f = jnp.broadcast_to(resets.astype(F32)[None, :], (heads, tokens))
    front = jnp.stack([decay_rates.T, resets_f, jnp.zeros_like(resets_f)], axis=1)
    betas = step_order(reflect_betas)
    back = jnp.stack([jnp.zeros_like(betas), jnp.zeros_like(betas), betas], axis=1)
    rows = jnp.concatenate([front, back], axis=2)
    rows = jnp.pad(rows, ((0, 0), (0, 5), (0, 0)))
    cols = rows.transpose(0, 2, 1)
    keys2 = reflect_keys.reshape(tokens, 2 * heads * width)
    values2 = reflect_values.reshape(tokens, 2 * heads * width)

    def whole(*shape):
        return pl.BlockSpec((1,) + shape, lambda h: (h,) + (0,) * len(shape))

    def column(offset):
        return pl.BlockSpec((tokens, width), lambda h: (0, h + offset))

    total = tokens + width
    y, r, m, o, b = pl.pallas_call(
        local_kernel,
        grid=(heads,),
        in_specs=[whole(8, tokens + steps), whole(tokens + steps, 8), column(0),
                  column(0), column(heads), column(0), column(heads)],
        out_specs=[whole(total, steps), whole(tokens, width), whole(width, width),
                   whole(tokens, width), whole(width, width)],
        out_shape=[jax.ShapeDtypeStruct((heads, total, steps), BF16),
                   jax.ShapeDtypeStruct((heads, tokens, width), BF16),
                   jax.ShapeDtypeStruct((heads, width, width), F32),
                   jax.ShapeDtypeStruct((heads, tokens, width), F32),
                   jax.ShapeDtypeStruct((heads, width, width), F32)],
        compiler_params=pltpu.CompilerParams(vmem_limit_bytes=48 << 20),
        cost_estimate=pl.CostEstimate(flops=8 << 30, bytes_accessed=8 << 20, transcendentals=0),
        name="local",
    )(rows, cols, queries, keys2, keys2, values2, values2)

    up, d = pl.pallas_call(
        adjoint_kernel,
        grid=(heads,),
        in_specs=[pl.BlockSpec(cot.shape, lambda h: (0, 0)),
                  pl.BlockSpec((width, out_weight.shape[1]), lambda h: (h, 0)),
                  whole(tokens, width)],
        out_specs=[whole(tokens, width), whole(width, width)],
        out_shape=[jax.ShapeDtypeStruct((heads, tokens, width), BF16),
                   jax.ShapeDtypeStruct((heads, width, width), F32)],
        compiler_params=pltpu.CompilerParams(vmem_limit_bytes=32 << 20),
        name="adjoint",
    )(cot, out_weight, r)

    batched = functools.partial(lax.dot_general, precision=lax.Precision.HIGH,
                                preferred_element_type=F32)
    state = jnp.zeros((heads, width, width), BF16)
    adjoint = jnp.zeros((heads, width, width), BF16)
    for hop in range(devices - 1):
        out = batched(m, state.astype(F32), (((2,), (1,)), ((0,), (0,)))) + b
        back_out = batched(m, adjoint.astype(F32), (((1,), (1,)), ((0,), (0,)))) + d
        state = state + lax.ppermute(out.astype(BF16), "seq", [(hop, hop + 1)])
        adjoint = adjoint + lax.ppermute(
            back_out.astype(BF16), "seq", [(devices - 1 - hop, devices - 2 - hop)])

    flat = jax.ShapeDtypeStruct((tokens, heads * width), F32)
    mixed, g0, g1 = pl.pallas_call(
        finish_kernel,
        grid=(heads,),
        in_specs=[whole(tokens, width), whole(tokens, width), whole(width, width),
                  whole(total, steps), whole(tokens, width), whole(width, width)],
        out_specs=[column(0), column(0), column(0)],
        out_shape=[jax.ShapeDtypeStruct((tokens, heads * width), BF16), flat, flat],
        compiler_params=pltpu.CompilerParams(vmem_limit_bytes=32 << 20),
        name="finish",
    )(r, o, state, y, up, adjoint)
    value_grads = jnp.stack([g0, g1], axis=1)

    partial = lax.dot_general(out_weight, mixed, (((0,), (1,)), ((), ())), preferred_element_type=F32)
    output = lax.psum_scatter(partial, ("section", "head"), scatter_dimension=0, tiled=True)
    return output.astype(BF16), value_grads


def solution(mesh):
    return jax.shard_map(
        per_device,
        mesh=mesh,
        in_specs=(
            P(("grp", "seq"), ("section", "head")),
            P(("grp", "seq"), None, ("section", "head")),
            P(("grp", "seq"), None, ("section", "head")),
            P(("grp", "seq"), None, ("section", "head")),
            P(("grp", "seq"), ("section", "head")),
            P(("grp", "seq")),
            P(("section", "head"), None),
            P(("grp", "seq"), ("section", "head")),
        ),
        out_specs=(
            P(("section", "head"), ("grp", "seq")),
            P(("grp", "seq"), None, ("section", "head")),
        ),
        check_vma=False,
    )
```

profile of v0, /device:TPU:0, one launch (start us, length us, event | category | flops | bytes accessed | tf_op | source)
XLA Modules:
  0.0 116.1 jit_solution(4261849378134796591)
XLA Ops:
  7.2 0.0 copy-start.9
  7.2 0.0 all-gather.2.cloned.1.call-start
  7.2 0.7 all-gather.2.cloned.1.call-update
  7.9 0.0 reduce-scatter.2.cloned.1.call-start
  8.0 0.8 reshape.13
  8.7 0.1 stack_reshape.3
  8.8 0.7 convert_element_type.30
  9.5 0.7 select_maximum_fusion
  10.3 0.0 copy-start.10
  10.3 0.5 copy.27
  10.8 0.5 copy.40
  11.3 0.0 copy-done.9
  11.3 0.1 copy.37
  11.4 0.0 copy-done.10
  11.4 0.0 copy-start.8
  11.4 0.1 copy.38
  11.5 0.1 pad_bitcast_fusion.cols_ref
  11.6 0.8 copy-done.8
  12.3 0.0 copy-start
  12.3 28.1 %local.1 = (bf16[4,384,512]{2,1,0:T(8,128)(2,1)S(1)}, bf16[4,256,128]{2,1,0:T(8,128)(2,1)S(1)}, f32[4,128,128]{2,1,0:T(8,128)S(1)}, f32[4,256,128]{2,1,0:T(8,128)S(1)}, f32[4,128,128]{2,1,0:T(8,128)S(1)}) custom-call(f32[4,8,768]{2,1,0:T(8,128)S(1)} %pad.5.clone.rows_ref, f32[4,768,8]{2,1,0:T(8,128)S(1)} %pad_bitcast_fusion.cols_ref, ...), custom_call_target="tpu_custom_call" | custom-call | flops 8589934592 | bytes 8388608 | tf_op jit(solution)/shard_map/local/pallas_call | solution.py:202
  40.4 0.0 copy-start.1
  40.4 1.2 copy-done.1
  41.6 0.2 fusion
  41.8 4.9 %collective-permute-start = (bf16[4,128,128]{2,1,0:T(8,128)(2,1)S(1)}, bf16[4,128,128]{2,1,0:T(8,128)(2,1)S(1)}, u32[]{:S(2)}, u32[]{:S(2)}) collective-permute-start(bf16[4,128,128]{2,1,0:T(8,128)(2,1)S(1)} %fusion), channel_id=1, source_target_pairs={{0,4},{1,5},{2,6},{3,7},{16,20},{17,21},{18,22},{19,23}} | collective-permute-start | bytes 393224 | tf_op jit(solution)/shard_map/ppermute | solution.py:239
  46.7 2.7 %collective-permute-done = bf16[4,128,128]{2,1,0:T(8,128)(2,1)S(1)} collective-permute-done((bf16[4,128,128]{2,1,0:T(8,128)(2,1)S(1)}, bf16[4,128,128]{2,1,0:T(8,128)(2,1)S(1)}, u32[]{:S(2)}, u32[]{:S(2)}) %collective-permute-start) | collective-permute-done | bytes 131104 | tf_op jit(solution)/shard_map/ppermute | solution.py:239
  49.5 0.9 fusion.1
  50.4 1.3 %collective-permute-start.1 = (bf16[4,128,128]{2,1,0:T(8,128)(2,1)}, bf16[4,128,128]{2,1,0:T(8,128)(2,1)}, u32[]{:S(2)}, u32[]{:S(2)}) collective-permute-start(bf16[4,128,128]{2,1,0:T(8,128)(2,1)} %fusion.1), channel_id=1, source_target_pairs={{4,8},{5,9},{6,10},{7,11},{20,24},{21,25},{22,26},{23,27}} | collective-permute-start | bytes 393224 | tf_op jit(solution)/shard_map/ppermute | solution.py:239
  51.7 0.0 all-gather.2.cloned.1.call-done.cot_ref
  51.7 0.0 copy-done
  51.7 0.0 copy-start.3
  51.7 1.2 %copy-done.3 = bf16[256,2048]{1,0:T(8,128)(2,1)S(1)} copy-done((bf16[256,2048]{1,0:T(8,128)(2,1)S(1)}, bf16[256,2048]{1,0:T(8,128)(2,1)}, u32[]{:S(2)}) %copy-start.3) | copy-done | bytes 1048600
  52.9 2.5 %adjoint.1 = (bf16[4,256,128]{2,1,0:T(8,128)(2,1)S(1)}, f32[4,128,128]{2,1,0:T(8,128)S(1)}) custom-call(bf16[256,2048]{1,0:T(8,128)(2,1)S(1)} %copy-done.3, bf16[512,2048]{1,0:T(8,128)(2,1)S(1)} %copy-done, bf16[4,256,128]{2,1,0:T(8,128)(2,1)S(1)} %get-tuple-element.12.r_ref), custom_call_target="tpu_custom_call" | custom-call | tf_op jit(solution)/shard_map/adjoint/pallas_call | solution.py:219
  55.4 0.4 fusion.3
  55.8 0.0 copy-start.2
  55.8 0.8 collective-permute-start.3
  56.6 0.0 collective-permute-done.1
  56.6 0.9 add.38
  57.5 0.0 collective-permute-done.3
  57.6 0.3 fusion.4
  57.9 0.7 collective-permute-start.4
  58.6 0.2 fusion.2
  58.8 0.7 collective-permute-start.2
  59.5 0.0 collective-permute-done.4
  59.5 0.3 fusion.5
  59.9 1.3 %collective-permute-start.5 = (bf16[4,128,128]{2,1,0:T(8,128)(2,1)S(1)}, bf16[4,128,128]{2,1,0:T(8,128)(2,1)S(1)}, u32[]{:S(2)}, u32[]{:S(2)}) collective-permute-start(bf16[4,128,128]{2,1,0:T(8,128)(2,1)S(1)} %fusion.5), channel_id=1, source_target_pairs={{4,0},{5,1},{6,2},{7,3},{20,16},{21,17},{22,18},{23,19}} | collective-permute-start | bytes 393224 | tf_op jit(solution)/shard_map/ppermute | solution.py:240
  61.2 0.0 collective-permute-done.2
  61.2 11.2 %collective-permute-done.5 = bf16[4,128,128]{2,1,0:T(8,128)(2,1)S(1)} collective-permute-done((bf16[4,128,128]{2,1,0:T(8,128)(2,1)S(1)}, bf16[4,128,128]{2,1,0:T(8,128)(2,1)S(1)}, u32[]{:S(2)}, u32[]{:S(2)}) %collective-permute-start.5) | collective-permute-done | bytes 131104 | tf_op jit(solution)/shard_map/ppermute | solution.py:240
  72.5 0.0 copy-done.2
  72.5 1.4 %finish.1 = (bf16[256,512]{1,0:T(8,128)(2,1)S(1)}, f32[256,512]{1,0:T(8,128)S(1)}, f32[256,512]{1,0:T(8,128)S(1)}) custom-call(bf16[4,256,128]{2,1,0:T(8,128)(2,1)S(1)} %get-tuple-element.12.r_ref, f32[4,256,128]{2,1,0:T(8,128)S(1)} %get-tuple-element.13.o_ref, bf16[4,128,128]{2,1,0:T(8,128)(2,1)S(1)} %add.40.s_ref, bf16[4,384,512]{2,1,0:T(8,128)(2,1)S(1)} %copy-done.2, ...), custom_call_target="tpu_custom_call" | custom-call | tf_op jit(solution)/shard_map/finish/pallas_call | solution.py:244
  73.9 0.0 copy-start.4
  74.0 0.8 copy-done.4
  74.7 0.0 copy-start.6
  74.7 0.8 copy-done.6
  75.5 2.0 %convolution_bitcast_fusion = f32[2048,256]{0,1:T(8,128)} fusion(bf16[256,512]{1,0:T(8,128)(2,1)S(1)} %get-tuple-element.19, bf16[512,2048]{1,0:T(8,128)(2,1)S(1)} %copy-done), kind=kOutput, calls=%fused_computation | convolution fusion | flops 536870912 | bytes 4456448 | tf_op jit(solution)/shard_map/dot_general | solution.py:256
  77.6 0.0 copy-start.5
  77.6 0.0 copy-start.7
  77.6 0.0 reduce-scatter.2.cloned.1.call-update
  77.6 1.0 copy-done.5
  78.6 0.2 copy-done.7
  78.8 0.1 pad_maximum_fusion
  78.8 1.8 %copy.33 = f32[256,2,512]{2,1,0:T(2,128)} copy(f32[256,2,512]{2,0,1:T(8,128)S(1)} %pad_maximum_fusion) | data formatting | bytes 2097152
  80.6 26.7 %reduce-scatter.2.cloned.1.call-done = f32[512,256]{0,1:T(8,128)} async-done(((f32[2048,256]{0,1:T(8,128)}), f32[512,256]{0,1:T(8,128)}) %reduce-scatter.2.cloned.1.call-update) | async-done | bytes 524304 | tf_op jit(solution)/shard_map/reduce_scatter | solution.py:257
  107.4 1.1 convert_element_type.37
  108.4 0.8 copy.32
  (8 shorter events, 0.2 us)
Async XLA Ops:
  7.2 4.1 %copy-start.9 = (bf16[256,2,512]{2,1,0:T(2,128)(2,1)S(1)}, bf16[256,2,512]{2,1,0:T(2,128)(2,1)}, u32[]{:S(2)}) copy-start(bf16[256,2,512]{2,1,0:T(2,128)(2,1)} %param.9) | copy-start | bytes 1572868
  7.2 44.5 %all-gather.2.cloned.1.call-start = ((), (), s32[]{:S(2)}) async-start(), calls=%async_computation.1 | async-start | bytes 1310720 | tf_op jit(solution)/shard_map/all_gather | solution.py:183
  7.9 99.4 %reduce-scatter.2.cloned.1.call-start = ((), (), s32[]{:S(2)}) async-start(), calls=%async_computation.2 | async-start | bytes 2621440 | tf_op jit(solution)/shard_map/reduce_scatter | solution.py:257
  10.3 1.1 copy-start.10
  11.4 1.0 copy-start.8
  12.3 39.3 %copy-start = (bf16[512,2048]{1,0:T(8,128)(2,1)S(1)}, bf16[512,2048]{1,0:T(8,128)(2,1)}, u32[]{:S(2)}) copy-start(bf16[512,2048]{1,0:T(8,128)(2,1)} %w_ref.1) | copy-start | bytes 6291460
  40.4 1.2 %copy-start.1 = (bf16[4,384,512]{2,1,0:T(8,128)(2,1)}, bf16[4,384,512]{2,1,0:T(8,128)(2,1)S(1)}, u32[]{:S(2)}) copy-start(bf16[4,384,512]{2,1,0:T(8,128)(2,1)S(1)} %get-tuple-element.16.y_ref) | copy-start | bytes 4718596
  41.8 7.7 %collective-permute-start = (bf16[4,128,128]{2,1,0:T(8,128)(2,1)S(1)}, bf16[4,128,128]{2,1,0:T(8,128)(2,1)S(1)}, u32[]{:S(2)}, u32[]{:S(2)}) collective-permute-start(bf16[4,128,128]{2,1,0:T(8,128)(2,1)S(1)} %fusion), channel_id=1, source_target_pairs={{0,4},{1,5},{2,6},{3,7},{16,20},{17,21},{18,22},{19,23}} | collective-permute-start | bytes 393224 | tf_op jit(solution)/shard_map/ppermute | solution.py:239
  50.4 6.2 %collective-permute-start.1 = (bf16[4,128,128]{2,1,0:T(8,128)(2,1)}, bf16[4,128,128]{2,1,0:T(8,128)(2,1)}, u32[]{:S(2)}, u32[]{:S(2)}) collective-permute-start(bf16[4,128,128]{2,1,0:T(8,128)(2,1)} %fusion.1), channel_id=1, source_target_pairs={{4,8},{5,9},{6,10},{7,11},{20,24},{21,25},{22,26},{23,27}} | collective-permute-start | bytes 393224 | tf_op jit(solution)/shard_map/ppermute | solution.py:239
  51.7 1.2 %copy-start.3 = (bf16[256,2048]{1,0:T(8,128)(2,1)S(1)}, bf16[256,2048]{1,0:T(8,128)(2,1)}, u32[]{:S(2)}) copy-start(bf16[256,2048]{1,0:T(8,128)(2,1)} %all-gather.2.cloned.1.call-done.cot_ref) | copy-start | bytes 3145732
  55.8 16.7 %copy-start.2 = (bf16[4,384,512]{2,1,0:T(8,128)(2,1)S(1)}, bf16[4,384,512]{2,1,0:T(8,128)(2,1)}, u32[]{:S(2)}) copy-start(bf16[4,384,512]{2,1,0:T(8,128)(2,1)} %copy-done.1) | copy-start | bytes 4718596
  55.8 1.8 %collective-permute-start.3 = (bf16[4,128,128]{2,1,0:T(8,128)(2,1)S(1)}, bf16[4,128,128]{2,1,0:T(8,128)(2,1)S(1)}, u32[]{:S(2)}, u32[]{:S(2)}) collective-permute-start(bf16[4,128,128]{2,1,0:T(8,128)(2,1)S(1)} %fusion.3), channel_id=1, source_target_pairs={{12,8},{13,9},{14,10},{15,11},{28,24},{29,25},{30,26},{31,27}} | collective-permute-start | bytes 393224 | tf_op jit(solution)/shard_map/ppermute | solution.py:240
  57.9 1.6 %collective-permute-start.4 = (bf16[4,128,128]{2,1,0:T(8,128)(2,1)S(1)}, bf16[4,128,128]{2,1,0:T(8,128)(2,1)S(1)}, u32[]{:S(2)}, u32[]{:S(2)}) collective-permute-start(bf16[4,128,128]{2,1,0:T(8,128)(2,1)S(1)} %fusion.4), channel_id=1, source_target_pairs={{8,4},{9,5},{10,6},{11,7},{24,20},{25,21},{26,22},{27,23}} | collective-permute-start | bytes 393224 | tf_op jit(solution)/shard_map/ppermute | solution.py:240
  58.8 2.4 %collective-permute-start.2 = (bf16[4,128,128]{2,1,0:T(8,128)(2,1)S(1)}, bf16[4,128,128]{2,1,0:T(8,128)(2,1)S(1)}, u32[]{:S(2)}, u32[]{:S(2)}) collective-permute-start(bf16[4,128,128]{2,1,0:T(8,128)(2,1)S(1)} %fusion.2), channel_id=1, source_target_pairs={{8,12},{9,13},{10,14},{11,15},{24,28},{25,29},{26,30},{27,31}} | collective-permute-start | bytes 393224 | tf_op jit(solution)/shard_map/ppermute | solution.py:239
  59.9 12.6 %collective-permute-start.5 = (bf16[4,128,128]{2,1,0:T(8,128)(2,1)S(1)}, bf16[4,128,128]{2,1,0:T(8,128)(2,1)S(1)}, u32[]{:S(2)}, u32[]{:S(2)}) collective-permute-start(bf16[4,128,128]{2,1,0:T(8,128)(2,1)S(1)} %fusion.5), channel_id=1, source_target_pairs={{4,0},{5,1},{6,2},{7,3},{20,16},{21,17},{22,18},{23,19}} | collective-permute-start | bytes 393224 | tf_op jit(solution)/shard_map/ppermute | solution.py:240
  73.9 0.8 copy-start.4
  74.7 0.8 copy-start.6
  77.6 1.0 copy-start.5
  77.6 1.2 %copy-start.7 = (f32[256,512]{1,0:T(8,128)S(1)}, f32[256,512]{1,0:T(8,128)}, u32[]{:S(2)}) copy-start(f32[256,512]{1,0:T(8,128)} %copy-done.6) | copy-start | bytes 1572868
Sparse Core Ops, SparseCore 0:
  9.6 19.4 all-gather.1
  77.7 29.5 reduce-scatter.1
where the time goes:
time: 117 us; the launch traced here: 116 us
  waiting for transfers between devices  41.4 us (35%)
  Pallas kernels  32 us (27%)
  between operations  14.3 us (12%)
  local copies, waits for them, and re-layouts  10.7 us (9%)
  starting transfers between devices  9.75 us (8%)
  matrix products  4.42 us (4%)
  other arithmetic  3.59 us (3%)
    pallas_call x1, Pallas kernels, per_device(): pl.pallas_call(local_kernel, grid=(heads,), in_specs=[whole(8, tokens + s...  28.1 us
    reduce_scatter x1, waiting for transfers between devices, per_device(): lax.psum_scatter(partial, ('section', 'head'), scatter_dimension=0, tiled...  26.7 us
    ppermute x3, waiting for transfers between devices, per_device(): lax.ppermute(back_out.astype(BF16), 'seq', [(devices - 1 - hop, devices -...  11.2 us
    unnamed x27, local copies, waits for them, and re-layouts  9.13 us
    ppermute x3, starting transfers between devices, per_device(): state = state + lax.ppermute(out.astype(BF16), 'seq', [(hop, hop + 1)])  6.91 us
    ppermute x3, starting transfers between devices, per_device(): lax.ppermute(back_out.astype(BF16), 'seq', [(devices - 1 - hop, devices -...  2.76 us
    ppermute x3, waiting for transfers between devices, per_device(): state = state + lax.ppermute(out.astype(BF16), 'seq', [(hop, hop + 1)])  2.74 us
    pallas_call x1, Pallas kernels, per_device(): pl.pallas_call(adjoint_kernel, grid=(heads,), in_specs=[pl.BlockSpec(cot....  2.47 us
  transfers between devices with their start and end apart: 8, of which 3 were waited for; matrix products, arithmetic and copies ran while one was open for 7% of the time, Pallas kernels for 26%

commit v1 on v0

--- a/solution.py
+++ b/solution.py
@@ -156,15 +156,161 @@
     d_ref[0] = dot1(r_ref[0], up, TN)
 
 
-def finish_kernel(r_ref, o_ref, s_ref, y_ref, up_ref, ds_ref, mixed_ref, g0_ref, g1_ref):
-    tokens, width = mixed_ref.shape
-    mixed_ref[...] = (dot1(r_ref[0], s_ref[0]) + o_ref[0]).astype(BF16)
-    right = jnp.concatenate([up_ref[0], ds_ref[0].astype(BF16)], axis=0)
-    grad = dot1(y_ref[0], right, TN)
-    for b in range(tokens // HALF):
-        t = slice(b * HALF, (b + 1) * HALF)
-        g0_ref[t, :] = grad[b * BLK:b * BLK + HALF]
-        g1_ref[t, :] = grad[b * BLK + HALF:(b + 1) * BLK]
+MESH = pl.DeviceIdType.MESH
+
+
+def chain_kernel(devices, m_ref, b_ref, d_ref, s_ref, ds_ref, s_in, s_out, ds_in, ds_out,
+                 s_sent, s_got, ds_sent, ds_got):
+    heads = m_ref.shape[0]
+    place = lax.axis_index("seq")
+    first, last = place == 0, place == devices - 1
+    barrier = pltpu.get_barrier_semaphore()
+
+    @pl.when(jnp.logical_not(first))
+    def _():
+        pl.semaphore_signal(barrier, inc=1, device_id={"seq": place - 1}, device_id_type=MESH)
+
+    @pl.when(jnp.logical_not(last))
+    def _():
+        pl.semaphore_signal(barrier, inc=1, device_id={"seq": place + 1}, device_id_type=MESH)
+
+    if devices > 1:
+        pl.semaphore_wait(barrier, jnp.where(first | last, 1, 2))
+
+    def up(h):
+        return pltpu.make_async_remote_copy(
+            src_ref=s_out.at[h], dst_ref=s_in.at[h], send_sem=s_sent.at[h], recv_sem=s_got.at[h],
+            device_id={"seq": place + 1}, device_id_type=MESH)
+
+    def down(h):
+        return pltpu.make_async_remote_copy(
+            src_ref=ds_out.at[h], dst_ref=ds_in.at[h], send_sem=ds_sent.at[h], recv_sem=ds_got.at[h],
+            device_id={"seq": place - 1}, device_id_type=MESH)
+
+    def forward():
+        for h in range(heads):
+            @pl.when(first)
+            def _():
+                s_in[h] = jnp.zeros(s_in.shape[1:], BF16)
+
+            @pl.when(jnp.logical_not(first))
+            def _():
+                up(h).wait_recv()
+
+            @pl.when(jnp.logical_not(last))
+            def _():
+                mh, ml = halves(m_ref[h])
+                s = s_in[h]
+                s_out[h] = (dot1(mh, s) + dot1(ml, s) + b_ref[h]).astype(BF16)
+                up(h).start()
+
+            s_ref[h] = s_in[h]
+
+    def backward():
+        for h in range(heads):
+            @pl.when(last)
+            def _():
+                ds_in[h] = jnp.zeros(ds_in.shape[1:], BF16)
+
+            @pl.when(jnp.logical_not(last))
+            def _():
+                down(h).wait_recv()
+
+            @pl.when(jnp.logical_not(first))
+            def _():
+                mh, ml = halves(m_ref[h])
+                ds = ds_in[h]
+                ds_out[h] = (dot1(mh, ds, TN) + dot1(ml, ds, TN) + d_ref[h]).astype(BF16)
+                down(h).start()
+
+            ds_ref[h] = ds_in[h]
+
+    low = 2 * place < devices
+
+    @pl.when(low)
+    def _():
+        forward()
+        backward()
+
+    @pl.when(jnp.logical_not(low))
+    def _():
+        backward()
+        forward()
+
+    @pl.when(jnp.logical_not(last))
+    def _():
+        for h in range(heads):
+            up(h).wait_send()
+
+    @pl.when(jnp.logical_not(first))
+    def _():
+        for h in range(heads):
+            down(h).wait_send()
+
+
+def output_kernel(sections, r_ref, o_ref, s_ref, y_ref, up_ref, ds_ref, w_ref,
+                  out_ref, g0_ref, g1_ref,
+                  mixed, pair_out, pair_in, cross_out, cross_in,
+                  pair_sent, pair_got, cross_sent, cross_got):
+    heads, tokens, width = r_ref.shape
+    features = out_ref.shape[0]
+    section, core = lax.axis_index("section"), lax.axis_index("head")
+    sibling = 1 - core
+
+    def peer(k):
+        return lax.rem(section + k, sections)
+
+    barrier = pltpu.get_barrier_semaphore()
+    pl.semaphore_signal(barrier, inc=1, device_id={"head": sibling}, device_id_type=MESH)
+    for k in range(1, sections):
+        pl.semaphore_signal(barrier, inc=1, device_id={"section": peer(k)}, device_id_type=MESH)
+
+    for h in range(heads):
+        mixed[h * width:(h + 1) * width, :] = (dot1(r_ref[h], s_ref[h]) + o_ref[h]).T.astype(BF16)
+    pl.semaphore_wait(barrier, sections)
+
+    def partial(target, side):
+        start = pl.multiple_of((target * 2 + side) * features, 128)
+        return dot1(w_ref[:, pl.ds(start, features)], mixed[...], TN)
+
+    def pair(k):
+        return pltpu.make_async_remote_copy(
+            src_ref=pair_out.at[k], dst_ref=pair_in.at[k], send_sem=pair_sent.at[k],
+            recv_sem=pair_got.at[k], device_id={"head": sibling}, device_id_type=MESH)
+
+    def cross(k):
+        return pltpu.make_async_remote_copy(
+            src_ref=cross_out.at[k - 1], dst_ref=cross_in.at[k - 1], send_sem=cross_sent.at[k - 1],
+            recv_sem=cross_got.at[k - 1], device_id={"section": peer(k)}, device_id_type=MESH)
+
+    order = list(range(1, sections)) + [0]
+    for k in order:
+        pair_out[k] = partial(peer(k), sibling)
+        pair(k).start()
+    for k in range(1, sections):
+        mine = partial(peer(k), core)
+        pair(k).wait_recv()
+        cross_out[k - 1] = (mine + pair_in[k]).astype(BF16)
+        cross(k).start()
+    for h in range(heads):
+        right = jnp.concatenate([up_ref[h], ds_ref[h]], axis=0)
+        grad = dot1(y_ref[h], right, TN)
+        lanes = slice(h * width, (h + 1) * width)
+        for b in range(tokens // HALF):
+            t = slice(b * HALF, (b + 1) * HALF)
+            g0_ref[t, lanes] = grad[b * BLK:b * BLK + HALF]
+            g1_ref[t, lanes] = grad[b * BLK + HALF:(b + 1) * BLK]
+    total = partial(section, core)
+    pair(0).wait_recv()
+    total = total + pair_in[0]
+    for k in range(1, sections):
+        cross(k).wait_recv()
+        total = total + cross_in[k - 1].astype(F32)
+    out_ref[...] = total.astype(BF16)
+    for k in order:
+        pair(k).wait_send()
+    for k in range(1, sections):
+        cross(k).wait_send()
 
 
 def step_order(array):
@@ -229,33 +375,39 @@
         name="adjoint",
     )(cot, out_weight, r)
 
-    batched = functools.partial(lax.dot_general, precision=lax.Precision.HIGH,
-                                preferred_element_type=F32)
-    state = jnp.zeros((heads, width, width), BF16)
-    adjoint = jnp.zeros((heads, width, width), BF16)
-    for hop in range(devices - 1):
-        out = batched(m, state.astype(F32), (((2,), (1,)), ((0,), (0,)))) + b
-        back_out = batched(m, adjoint.astype(F32), (((1,), (1,)), ((0,), (0,)))) + d
-        state = state + lax.ppermute(out.astype(BF16), "seq", [(hop, hop + 1)])
-        adjoint = adjoint + lax.ppermute(
-            back_out.astype(BF16), "seq", [(devices - 1 - hop, devices - 2 - hop)])
-
+    square = (heads, width, width)
+    vmem = pl.BlockSpec(memory_space=pltpu.VMEM)
+    dma = pltpu.SemaphoreType.DMA
+    state, adjoint = pl.pallas_call(
+        functools.partial(chain_kernel, devices),
+        in_specs=[vmem] * 3,
+        out_specs=[vmem] * 2,
+        out_shape=[jax.ShapeDtypeStruct(square, BF16)] * 2,
+        scratch_shapes=[pltpu.VMEM(square, BF16)] * 4 + [dma((heads,))] * 4,
+        compiler_params=pltpu.CompilerParams(
+            collective_id=0, has_side_effects=True, vmem_limit_bytes=32 << 20),
+        name="chain",
+    )(m, b, d)
+
+    sections = lax.axis_size("section")
+    features = out_weight.shape[1] // (2 * sections)
     flat = jax.ShapeDtypeStruct((tokens, heads * width), F32)
-    mixed, g0, g1 = pl.pallas_call(
-        finish_kernel,
-        grid=(heads,),
-        in_specs=[whole(tokens, width), whole(tokens, width), whole(width, width),
-                  whole(total, steps), whole(tokens, width), whole(width, width)],
-        out_specs=[column(0), column(0), column(0)],
-        out_shape=[jax.ShapeDtypeStruct((tokens, heads * width), BF16), flat, flat],
-        compiler_params=pltpu.CompilerParams(vmem_limit_bytes=32 << 20),
-        name="finish",
-    )(r, o, state, y, up, adjoint)
-    value_grads = jnp.stack([g0, g1], axis=1)
-
-    partial = lax.dot_general(out_weight, mixed, (((0,), (1,)), ((), ())), preferred_element_type=F32)
-    output = lax.psum_scatter(partial, ("section", "head"), scatter_dimension=0, tiled=True)
-    return output.astype(BF16), value_grads
+    output, g0, g1 = pl.pallas_call(
+        functools.partial(output_kernel, sections),
+        in_specs=[vmem] * 7,
+        out_specs=[vmem] * 3,
+        out_shape=[jax.ShapeDtypeStruct((features, tokens), BF16), flat, flat],
+        scratch_shapes=[pltpu.VMEM((heads * width, tokens), BF16),
+                        pltpu.VMEM((sections, features, tokens), F32),
+                        pltpu.VMEM((sections, features, tokens), F32),
+                        pltpu.VMEM((sections - 1, features, tokens), BF16),
+                        pltpu.VMEM((sections - 1, features, tokens), BF16),
+                        dma((sections,)), dma((sections,)), dma((sections - 1,)), dma((sections - 1,))],
+        compiler_params=pltpu.CompilerParams(
+            collective_id=1, has_side_effects=True, vmem_limit_bytes=48 << 20),
+        name="output",
+    )(r, o, state, y, up, adjoint, out_weight)
+    return output, jnp.stack([g0, g1], axis=1)
 
 
 def solution(mesh):

time: 117 us -> 82.9 us (0.71)
  waiting for transfers between devices: 41.4 us -> 0.68 us
  Pallas kernels: 32 us -> 57.9 us
  starting transfers between devices: 9.75 us -> 0.04 us
  matrix products: 4.42 us -> 0 us
  local copies, waits for them, and re-layouts: 10.7 us -> 8.34 us
  other arithmetic: 3.59 us -> 1.46 us
    reduce_scatter x1 -> x0, waiting for transfers between devices: 26.7 us -> none  [per_device(): lax.psum_scatter(partial, ('section', 'head'), scatter_dimension=0, tiled...]
    pallas_call x1 -> x2, Pallas kernels: 1.43 us -> 27.3 us  [the longest x1 14.4 us: per_device(): pl.pallas_call(functools.partial(chain_kernel, devices), in_specs=[vmem]...]
    ppermute x6 -> x0, waiting for transfers between devices: 14 us -> none  [the longest x3 11.2 us: per_device(): lax.ppermute(back_out.astype(BF16), 'seq', [(devices - 1 - hop, devices -...]
    ppermute x6 -> x0, starting transfers between devices: 9.68 us -> none  [the longest x3 6.91 us: per_device(): state = state + lax.ppermute(out.astype(BF16), 'seq', [(hop, hop + 1)])]
    dot_general x7 -> x0, matrix products: 4.42 us -> none  [the longest x1 2.04 us: per_device(): lax.dot_general(out_weight, mixed, (((0,), (1,)), ((), ())), preferred_el...]
    unnamed x27 -> x19, local copies, waits for them, and re-layouts: 9.13 us -> 6.81 us
  transfers between devices with their start and end apart: 8 -> 1, of which waited for: 3 -> 0; matrix products, arithmetic and copies ran while one was open for 7% -> 4% of each run, Pallas kernels for 26% -> 34%
where the time goes in v1:
time: 82.9 us; the launch traced here: 82.5 us
  Pallas kernels  57.9 us (70%)
  between operations  14.2 us (17%)
  local copies, waits for them, and re-layouts  8.34 us (10%)
  other arithmetic  1.46 us (2%)
    pallas_call x1, Pallas kernels, per_device(): pl.pallas_call(local_kernel, grid=(heads,), in_specs=[whole(8, tokens + s...  28.1 us
    pallas_call x1, Pallas kernels, per_device(): pl.pallas_call(functools.partial(chain_kernel, devices), in_specs=[vmem]...  14.4 us
    pallas_call x1, Pallas kernels, per_device(): pl.pallas_call(functools.partial(output_kernel, sections), in_specs=[vmem...  12.9 us
    unnamed x19, local copies, waits for them, and re-layouts  6.81 us
    pallas_call x1, Pallas kernels, per_device(): pl.pallas_call(adjoint_kernel, grid=(heads,), in_specs=[pl.BlockSpec(cot....  2.47 us
  transfers between devices with their start and end apart: 1, of which 0 were waited for; matrix products, arithmetic and copies ran while one was open for 4% of the time, Pallas kernels for 34%

profile of v1, /device:TPU:0, one launch (start us, length us, event | category | flops | bytes accessed | tf_op | source)
XLA Modules:
  0.0 82.5 jit_solution(10403476168435713753)
XLA Ops:
  7.2 0.0 all-gather.2.cloned.1.call-start
  7.2 0.7 all-gather.2.cloned.1.call-update
  7.9 0.8 reshape.13
  8.7 0.1 stack_reshape.3
  8.8 0.7 convert_element_type.5
  9.5 0.7 select_maximum_fusion
  10.2 0.0 copy-start.5
  10.2 0.5 copy.19
  10.7 0.0 copy-start.6
  10.7 0.5 copy.25
  11.2 0.0 copy-done.5
  11.2 0.1 copy.22
  11.3 0.5 copy-done.6
  11.8 0.1 copy.23
  11.9 0.0 copy-start.4
  11.9 0.1 pad_bitcast_fusion.cols_ref
  12.0 0.8 %copy-done.4 = bf16[256,512]{1,0:T(8,128)(2,1)S(1)} copy-done((bf16[256,512]{1,0:T(8,128)(2,1)S(1)}, bf16[256,512]{1,0:T(8,128)(2,1)}, u32[]{:S(2)}) %copy-start.4) | copy-done | bytes 262168
  12.8 0.0 copy-start
  12.8 28.1 %local.1 = (bf16[4,384,512]{2,1,0:T(8,128)(2,1)S(1)}, bf16[4,256,128]{2,1,0:T(8,128)(2,1)S(1)}, f32[4,128,128]{2,1,0:T(8,128)S(1)}, f32[4,256,128]{2,1,0:T(8,128)S(1)}, f32[4,128,128]{2,1,0:T(8,128)S(1)}) custom-call(f32[4,8,768]{2,1,0:T(8,128)S(1)} %pad.5.clone.rows_ref, f32[4,768,8]{2,1,0:T(8,128)S(1)} %pad_bitcast_fusion.cols_ref, ...), custom_call_target="tpu_custom_call" | custom-call | flops 8589934592 | bytes 8388608 | tf_op jit(solution)/shard_map/local/pallas_call | solution.py:348
  40.9 0.0 copy-start.1
  40.9 1.2 %copy-done.1 = bf16[4,384,512]{2,1,0:T(8,128)(2,1)} copy-done((bf16[4,384,512]{2,1,0:T(8,128)(2,1)}, bf16[4,384,512]{2,1,0:T(8,128)(2,1)S(1)}, u32[]{:S(2)}) %copy-start.1) | copy-done | bytes 1572888
  42.1 0.0 all-gather.2.cloned.1.call-done.cot_ref
  42.1 0.0 copy-done
  42.1 0.0 copy-start.3
  42.1 1.2 %copy-done.3 = bf16[256,2048]{1,0:T(8,128)(2,1)S(1)} copy-done((bf16[256,2048]{1,0:T(8,128)(2,1)S(1)}, bf16[256,2048]{1,0:T(8,128)(2,1)}, u32[]{:S(2)}) %copy-start.3) | copy-done | bytes 1048600
  43.3 0.0 copy-start.2
  43.3 2.5 %adjoint.1 = (bf16[4,256,128]{2,1,0:T(8,128)(2,1)S(1)}, f32[4,128,128]{2,1,0:T(8,128)S(1)}) custom-call(bf16[256,2048]{1,0:T(8,128)(2,1)S(1)} %copy-done.3, bf16[512,2048]{1,0:T(8,128)(2,1)S(1)} %copy-done, bf16[4,256,128]{2,1,0:T(8,128)(2,1)S(1)} %get-tuple-element.14.r_ref), custom_call_target="tpu_custom_call" | custom-call | tf_op jit(solution)/shard_map/adjoint/pallas_call | solution.py:365
  45.8 14.4 %chain.1 = (bf16[4,128,128]{2,1,0:T(8,128)(2,1)S(1)}, bf16[4,128,128]{2,1,0:T(8,128)(2,1)S(1)}) custom-call(f32[4,128,128]{2,1,0:T(8,128)S(1)} %get-tuple-element.16.m_ref, f32[4,128,128]{2,1,0:T(8,128)S(1)} %get-tuple-element.17.b_ref, f32[4,128,128]{2,1,0:T(8,128)S(1)} %get-tuple-element.18.d_ref), custom_call_target="tpu_custom_call" | custom-call | tf_op jit(solution)/shard_map/chain/pallas_call | solution.py:381
  60.2 0.0 copy-done.2
  60.2 12.9 %output.1 = (bf16[512,256]{1,0:T(8,128)(2,1)S(1)}, f32[256,512]{1,0:T(8,128)S(1)}, f32[256,512]{1,0:T(8,128)S(1)}) custom-call(bf16[4,256,128]{2,1,0:T(8,128)(2,1)S(1)} %get-tuple-element.14.r_ref, f32[4,256,128]{2,1,0:T(8,128)S(1)} %get-tuple-element.15.o_ref, bf16[4,128,128]{2,1,0:T(8,128)(2,1)S(1)} %get-tuple-element.19.s_ref, ...), custom_call_target="tpu_custom_call" | custom-call | tf_op jit(solution)/shard_map/output/pallas_call | solution.py:395
  73.1 0.1 pad_maximum_fusion
  73.2 1.8 %copy.21 = f32[256,2,512]{2,1,0:T(2,128)} copy(f32[256,2,512]{2,0,1:T(8,128)S(1)} %pad_maximum_fusion) | data formatting | bytes 2097152
  75.0 0.7 copy.28
  (5 shorter events, 0.0 us)
Async XLA Ops:
  7.2 34.9 %all-gather.2.cloned.1.call-start = ((), (), s32[]{:S(2)}) async-start(), calls=%async_computation | async-start | bytes 1310720 | tf_op jit(solution)/shard_map/all_gather | solution.py:329
  10.2 1.0 %copy-start.5 = (bf16[256,2,512]{2,1,0:T(2,128)(2,1)S(1)}, bf16[256,2,512]{2,1,0:T(2,128)(2,1)}, u32[]{:S(2)}) copy-start(bf16[256,2,512]{2,1,0:T(2,128)(2,1)} %param.9) | copy-start | bytes 1572868
  10.7 1.1 %copy-start.6 = (bf16[256,2,512]{2,1,0:T(2,128)(2,1)S(1)}, bf16[256,2,512]{2,1,0:T(2,128)(2,1)}, u32[]{:S(2)}) copy-start(bf16[256,2,512]{2,1,0:T(2,128)(2,1)} %param.10) | copy-start | bytes 1572868
  11.9 1.0 %copy-start.4 = (bf16[256,512]{1,0:T(8,128)(2,1)S(1)}, bf16[256,512]{1,0:T(8,128)(2,1)}, u32[]{:S(2)}) copy-start(bf16[256,512]{1,0:T(8,128)(2,1)} %q_ref.1) | copy-start | bytes 786436
  12.8 29.2 %copy-start = (bf16[512,2048]{1,0:T(8,128)(2,1)S(1)}, bf16[512,2048]{1,0:T(8,128)(2,1)}, u32[]{:S(2)}) copy-start(bf16[512,2048]{1,0:T(8,128)(2,1)} %w_ref.3) | copy-start | bytes 6291460
  40.9 1.2 %copy-start.1 = (bf16[4,384,512]{2,1,0:T(8,128)(2,1)}, bf16[4,384,512]{2,1,0:T(8,128)(2,1)S(1)}, u32[]{:S(2)}) copy-start(bf16[4,384,512]{2,1,0:T(8,128)(2,1)S(1)} %get-tuple-element.20.y_ref) | copy-start | bytes 4718596
  42.1 1.2 %copy-start.3 = (bf16[256,2048]{1,0:T(8,128)(2,1)S(1)}, bf16[256,2048]{1,0:T(8,128)(2,1)}, u32[]{:S(2)}) copy-start(bf16[256,2048]{1,0:T(8,128)(2,1)} %all-gather.2.cloned.1.call-done.cot_ref) | copy-start | bytes 3145732
  43.3 16.9 %copy-start.2 = (bf16[4,384,512]{2,1,0:T(8,128)(2,1)S(1)}, bf16[4,384,512]{2,1,0:T(8,128)(2,1)}, u32[]{:S(2)}) copy-start(bf16[4,384,512]{2,1,0:T(8,128)(2,1)} %copy-done.1) | copy-start | bytes 4718596
Sparse Core Ops, SparseCore 0:
  9.6 19.4 all-gather.1

commit v2 on v1

--- a/solution.py
+++ b/solution.py
@@ -40,114 +40,142 @@
     return block * HALF + rest % HALF, rest // HALF
 
 
-def local_kernel(rows_ref, cols_ref, q_ref, k0_ref, k1_ref, v0_ref, v1_ref,
+def local_kernel(rows_ref, q_ref, k0_ref, k1_ref, v0_ref, v1_ref,
                  y_ref, r_ref, m_ref, o_ref, b_ref):
-    tokens, width = q_ref.shape
+    group, width = m_ref.shape[0], m_ref.shape[1]
+    tokens = q_ref.shape[0]
     blocks = tokens // HALF
     steps = 2 * tokens
-    rows, cols = rows_ref[0], cols_ref[0]
+    everything = [(g, b) for g in range(group) for b in range(blocks)]
+    rows = rows_ref[0]
+    top = rows.astype(BF16)
+    rest = rows - top.astype(F32)
+    middle = rest.astype(BF16)
+    bottom = (rest - middle.astype(F32)).astype(BF16)
     tok_s, ref_s = step_token(iota((tokens, steps), 1))
     source = iota((tokens, steps), 0)
     upto = (source <= tok_s).astype(F32)
-    before = jnp.where(ref_s == 1, upto, (source < tok_s).astype(F32))
-    high = functools.partial(lax.dot_general, precision=lax.Precision.HIGHEST,
-                             preferred_element_type=F32)
-    c_row = high(rows[:, :tokens], before, NN)[0:1]
-    z_row = high(rows[:, :tokens], upto, NN)[1:2]
-    beta_row = rows[2:3, tokens:]
-    tok_c, ref_c = step_token(iota((steps, tokens), 0))
-    source_c = iota((steps, tokens), 1)
-    upto_c = (source_c <= tok_c).astype(F32)
-    before_c = jnp.where(ref_c == 1, upto_c, (source_c < tok_c).astype(F32))
-    c_col = high(before_c, cols[:tokens], NN)[:, 0:1]
-    z_col = high(upto_c, cols[:tokens], NN)[:, 1:2]
-    beta_col = cols[tokens:, 2:3]
-    c_end, z_end = c_row[:, steps - 1:], z_row[:, steps - 1:]
-    gamma_row = jnp.where(z_row == 0, jnp.exp(-c_row), 0.0)
-    gamma_end_row = jnp.where(z_row == z_end, jnp.exp(c_row - c_end), 0.0)
-    gamma_end = jnp.where(z_end == 0, jnp.exp(-c_end), 0.0)
+    before = (source <= tok_s + ref_s - 1).astype(F32)
+    sums = dot1(jnp.concatenate([top.astype(F32), middle.astype(F32), bottom.astype(F32)], axis=0), before)
+    c_rows = sums[0:8] + sums[8:16] + sums[16:24]
+    z_rows = dot1(rows, upto)
+    beta_rows = []
+    for g in range(group):
+        first, second = rows[1 + group + g:2 + group + g], rows[1 + 2 * group + g:2 + 2 * group + g]
+        pieces = []
+        for b in range(blocks):
+            t = slice(b * HALF, (b + 1) * HALF)
+            pieces += [first[:, t], second[:, t]]
+        beta_rows.append(jnp.concatenate(pieces, axis=1))
+    z_row = z_rows[group:group + 1]
+    packed = jnp.concatenate(
+        [c_rows[0:group], z_row] + beta_rows + [jnp.zeros((7 - 2 * group, steps), F32)], axis=0)
+    packed_cols = packed.T
+    z_col = packed_cols[:, group:group + 1]
+    c_row = [c_rows[g:g + 1] for g in range(group)]
+    c_col = [packed_cols[:, g:g + 1] for g in range(group)]
+    beta_col = [packed_cols[:, group + 1 + g:group + 2 + g] for g in range(group)]
+    z_end = z_row[:, steps - 1:]
 
     def sl(b):
         return slice(b * BLK, (b + 1) * BLK)
 
-    keys, values = [], []
-    for b in range(blocks):
+    def lanes(g):
+        return slice(g * width, (g + 1) * width)
+
+    keys, values = {}, {}
+    for g, b in everything:
         t = slice(b * HALF, (b + 1) * HALF)
-        keys.append(jnp.concatenate([k0_ref[t, :], k1_ref[t, :]], axis=0))
-        values.append(jnp.concatenate([v0_ref[t, :], v1_ref[t, :]], axis=0))
+        keys[g, b] = jnp.concatenate([k0_ref[t, lanes(g)], k1_ref[t, lanes(g)]], axis=0)
+        values[g, b] = jnp.concatenate([v0_ref[t, lanes(g)], v1_ref[t, lanes(g)]], axis=0)
     eye = iota((BLK, BLK), 0) == iota((BLK, BLK), 1)
+    identity = jnp.where(eye, 1.0, 0.0)
     tm_r = 2 * (iota((BLK, BLK), 0) % HALF) + iota((BLK, BLK), 0) // HALF
     tm_c = 2 * (iota((BLK, BLK), 1) % HALF) + iota((BLK, BLK), 1) // HALF
 
-    gram = [[dot1(keys[b], keys[c], NT) for c in range(b + 1)] for b in range(blocks)]
-    scale_row, scale_col = [], []
-    for b in range(blocks):
-        diag = jnp.where(eye, gram[b][b], 0.0)
-        scale_row.append(lax.rsqrt(jnp.sum(diag, axis=0, keepdims=True) + 1e-6))
-        scale_col.append(lax.rsqrt(jnp.sum(diag, axis=1, keepdims=True) + 1e-6))
-
-    low = [[None] * blocks for _ in range(blocks)]
-    for b in range(blocks):
-        left = beta_col[sl(b)] * scale_col[b]
+    low, scale_row, scale_col, gram = {}, {}, {}, {}
+    for g, b in everything:
+        for c in range(b + 1):
+            gram[g, b, c] = dot1(keys[g, b], keys[g, c], NT)
+    for g, b in everything:
+        diag = jnp.where(eye, gram[g, b, b], 0.0)
+        scale_row[g, b] = lax.rsqrt(jnp.sum(diag, axis=0, keepdims=True) + 1e-6)
+        scale_col[g, b] = lax.rsqrt(jnp.sum(diag, axis=1, keepdims=True) + 1e-6)
+    for g, b in everything:
+        left = beta_col[g][sl(b)] * scale_col[g, b]
         for c in range(b + 1):
             valid = z_col[sl(b)] == z_row[:, sl(c)]
             if b == c:
                 valid = valid & (tm_r > tm_c)
-            gap = jnp.where(valid, c_row[:, sl(c)] - c_col[sl(b)], 0.0)
-            low[b][c] = jnp.where(valid, jnp.exp(gap) * gram[b][c] * left * scale_row[c], 0.0)
-
-    inverse = [jnp.where(eye, 1.0, 0.0) - jnp.where((tm_r >> 1) == (tm_c >> 1), low[b][b], 0.0)
-               for b in range(blocks)]
+            gap = jnp.where(valid, c_row[g][:, sl(c)] - c_col[g][sl(b)], 0.0)
+            low[g, b, c] = jnp.where(
+                valid, jnp.exp(gap) * gram[g, b, c] * left * scale_row[g, c], 0.0)
+
+    rounded = {i: low[i[0], i[1], i[1]].astype(BF16) for i in everything}
+    inverse = {i: identity - jnp.where((tm_r >> 1) == (tm_c >> 1), low[i[0], i[1], i[1]], 0.0)
+               for i in everything}
     level = 2
     while (1 << level) <= BLK:
         pick = ((tm_r >> level) == (tm_c >> level)) & ((tm_r >> (level - 1)) != (tm_c >> (level - 1)))
-        inner = [dot3(jnp.where(pick, low[b][b], 0.0), inverse[b]) for b in range(blocks)]
-        inverse = [inverse[b] - dot3(inverse[b], inner[b]) for b in range(blocks)]
+        narrow = {i: inverse[i].astype(BF16) for i in everything}
+        inner = {i: dot1(jnp.where(pick, rounded[i], jnp.zeros_like(rounded[i])), narrow[i])
+                 for i in everything}
+        inverse = {i: inverse[i] - dot1(narrow[i], inner[i]) for i in everything}
         level += 1
-
-    solved = [None] * blocks
+    for _ in range(2):
+        residual = {i: dot3(low[i[0], i[1], i[1]], inverse[i]) + (inverse[i] - identity)
+                    for i in everything}
+        inverse = {i: inverse[i] - dot1(inverse[i], residual[i]) for i in everything}
+
+    gamma_end_row = [jnp.where(z_row == z_end, jnp.exp(c_row[g] - c_row[g][:, steps - 1:]), 0.0)
+                     for g in range(group)]
+    solved = {}
     for b in reversed(range(blocks)):
-        parts = []
-        kq_scale = scale_row[b]
-        for a in range(b, blocks):
-            t = slice(a * HALF, (a + 1) * HALF)
-            product = dot1(q_ref[t, :], keys[b], NT)
-            second = slice(a * BLK + HALF, (a + 1) * BLK)
-            valid = z_col[second] == z_row[:, sl(b)]
-            if a == b:
-                valid = valid & (iota((HALF, BLK), 0) >= iota((HALF, BLK), 1) % HALF)
-            gap = jnp.where(valid, c_row[:, sl(b)] - c_col[second], 0.0)
-            parts.append(jnp.where(valid, jnp.exp(gap) * product * kq_scale, 0.0))
-        parts.append(keys[b].astype(F32).T * (kq_scale * gamma_end_row[:, sl(b)]))
-        x = jnp.concatenate(parts, axis=0)
-        if b + 1 < blocks:
-            later = []
-            for c in range(b + 1, blocks):
-                y = solved[c]
-                later.append(jnp.concatenate([jnp.zeros(((c - b) * HALF, BLK), F32), y], axis=0))
-            x = x - dot3(jnp.concatenate(later, axis=1),
-                         jnp.concatenate([low[c][b] for c in range(b + 1, blocks)], axis=0))
-        solved[b] = dot3(x, inverse[b])
+        for g in range(group):
+            parts = []
+            for a in range(b, blocks):
+                t = slice(a * HALF, (a + 1) * HALF)
+                product = dot1(q_ref[t, lanes(g)], keys[g, b], NT)
+                second = slice(a * BLK + HALF, (a + 1) * BLK)
+                valid = z_col[second] == z_row[:, sl(b)]
+                if a == b:
+                    valid = valid & (iota((HALF, BLK), 0) >= iota((HALF, BLK), 1) % HALF)
+                gap = jnp.where(valid, c_row[g][:, sl(b)] - c_col[g][second], 0.0)
+                parts.append(jnp.where(valid, jnp.exp(gap) * product * scale_row[g, b], 0.0))
+            parts.append(keys[g, b].astype(F32).T * (scale_row[g, b] * gamma_end_row[g][:, sl(b)]))
+            x = jnp.concatenate(parts, axis=0)
+            if b + 1 < blocks:
+                later = []
+                for c in range(b + 1, blocks):
+                    later.append(jnp.concatenate(
+                        [jnp.zeros(((c - b) * HALF, BLK), F32), solved[g, c]], axis=0))
+                x = x - dot3(jnp.concatenate(later, axis=1),
+                             jnp.concatenate([low[g, c, b] for c in range(b + 1, blocks)], axis=0))
+            solved[g, b] = dot3(x, inverse[g, b])
 
     total = tokens + width
-    plain = jnp.zeros((total, width), F32)
-    moved = jnp.zeros((total, width), F32)
-    for b in range(blocks):
-        y = solved[b] * beta_row[:, sl(b)]
-        if b:
-            y = jnp.concatenate([jnp.zeros((b * HALF, BLK), F32), y], axis=0)
-        y_ref[0, :, sl(b)] = y.astype(BF16)
-        plain = plain + dot1(y, values[b])
-        moved = moved + dot1(y * (gamma_row[:, sl(b)] * scale_row[b]), keys[b])
-    o_ref[0] = plain[:tokens]
-    b_ref[0] = plain[tokens:]
-    gamma_tok = []
-    for a in range(blocks):
-        second = slice(a * BLK + HALF, (a + 1) * BLK)
-        gamma_tok.append(jnp.where(z_col[second] == 0, jnp.exp(-c_col[second]), 0.0))
-    gamma_tok = jnp.concatenate(gamma_tok, axis=0)
-    r_ref[0] = (gamma_tok * q_ref[...].astype(F32) - moved[:tokens]).astype(BF16)
-    m_ref[0] = jnp.where(iota((width, width), 0) == iota((width, width), 1), gamma_end, 0.0) - moved[tokens:]
+    for g in range(group):
+        gamma_row = jnp.where(z_row == 0, jnp.exp(-c_row[g]), 0.0)
+        plain, moved, gamma_tok = [], [], []
+        for b in range(blocks):
+            y = solved[g, b] * packed[group + 1 + g:group + 2 + g, sl(b)]
+            if b:
+                y = jnp.concatenate([jnp.zeros((b * HALF, BLK), F32), y], axis=0)
+            y_ref[g, :, sl(b)] = y.astype(BF16)
+            plain.append(y.astype(BF16))
+            moved.append((y * (gamma_row[:, sl(b)] * scale_row[g, b])).astype(BF16))
+            second = slice(b * BLK + HALF, (b + 1) * BLK)
+            gamma_tok.append(jnp.where(z_col[second] == 0, jnp.exp(-c_col[g][second]), 0.0))
+        plain = dot1(jnp.concatenate(plain, axis=1),
+                     jnp.concatenate([values[g, b] for b in range(blocks)], axis=0))
+        moved = dot1(jnp.concatenate(moved, axis=1),
+                     jnp.concatenate([keys[g, b] for b in range(blocks)], axis=0))
+        o_ref[g] = plain[:tokens]
+        b_ref[g] = plain[tokens:]
+        gamma_tok = jnp.concatenate(gamma_tok, axis=0)
+        r_ref[g] = (gamma_tok * q_ref[:, lanes(g)].astype(F32) - moved[:tokens]).astype(BF16)
+        gamma_end = jnp.where(z_end == 0, jnp.exp(-c_row[g][:, steps - 1:]), 0.0)
+        m_ref[g] = jnp.where(iota((width, width), 0) == iota((width, width), 1), gamma_end, 0.0) - moved[tokens:]
 
 
 def adjoint_kernel(cot_ref, w_ref, r_ref, up_ref, d_ref):
@@ -249,7 +277,7 @@
 
 
 def output_kernel(sections, r_ref, o_ref, s_ref, y_ref, up_ref, ds_ref, w_ref,
-                  out_ref, g0_ref, g1_ref,
+                  out_ref, g_ref,
                   mixed, pair_out, pair_in, cross_out, cross_in,
                   pair_sent, pair_got, cross_sent, cross_got):
     heads, tokens, width = r_ref.shape
@@ -298,8 +326,8 @@
         lanes = slice(h * width, (h + 1) * width)
         for b in range(tokens // HALF):
             t = slice(b * HALF, (b + 1) * HALF)
-            g0_ref[t, lanes] = grad[b * BLK:b * BLK + HALF]
-            g1_ref[t, lanes] = grad[b * BLK + HALF:(b + 1) * BLK]
+            g_ref[t, 0, lanes] = grad[b * BLK:b * BLK + HALF]
+            g_ref[t, 1, lanes] = grad[b * BLK + HALF:(b + 1) * BLK]
     total = partial(section, core)
     pair(0).wait_recv()
     total = total + pair_in[0]
@@ -313,11 +341,6 @@
         cross(k).wait_send()
 
 
-def step_order(array):
-    tokens, _, heads = array.shape
-    return array.reshape(tokens // HALF, HALF, 2, heads).transpose(3, 0, 2, 1).reshape(heads, 2 * tokens)
-
-
 def per_device(queries, reflect_keys, reflect_values, reflect_betas, decay_rates, resets,
                out_weight, out_cotangent):
     tokens = queries.shape[0]
@@ -328,30 +351,32 @@
 
     cot = lax.all_gather(out_cotangent, ("section", "head"), axis=1, tiled=True)
 
-    resets_f = jnp.broadcast_to(resets.astype(F32)[None, :], (heads, tokens))
-    front = jnp.stack([decay_rates.T, resets_f, jnp.zeros_like(resets_f)], axis=1)
-    betas = step_order(reflect_betas)
-    back = jnp.stack([jnp.zeros_like(betas), jnp.zeros_like(betas), betas], axis=1)
-    rows = jnp.concatenate([front, back], axis=2)
-    rows = jnp.pad(rows, ((0, 0), (0, 5), (0, 0)))
-    cols = rows.transpose(0, 2, 1)
+    group = 2 if heads % 2 == 0 else 1
+    groups = heads // group
+    marks = jnp.broadcast_to(resets.astype(F32)[None, None, :], (groups, 1, tokens))
+    betas = reflect_betas.transpose(1, 2, 0).reshape(2, groups, group, tokens)
+    rows = jnp.concatenate(
+        [decay_rates.T.reshape(groups, group, tokens), marks, betas[0], betas[1],
+         jnp.zeros((groups, 7 - 3 * group, tokens), F32)], axis=1)
     keys2 = reflect_keys.reshape(tokens, 2 * heads * width)
     values2 = reflect_values.reshape(tokens, 2 * heads * width)
 
     def whole(*shape):
         return pl.BlockSpec((1,) + shape, lambda h: (h,) + (0,) * len(shape))
 
-    def column(offset):
-        return pl.BlockSpec((tokens, width), lambda h: (0, h + offset))
+    def several(*shape):
+        return pl.BlockSpec((group,) + shape, lambda h: (h,) + (0,) * len(shape))
+
+    def columns(offset):
+        return pl.BlockSpec((tokens, group * width), lambda h: (0, h + offset))
 
     total = tokens + width
     y, r, m, o, b = pl.pallas_call(
         local_kernel,
-        grid=(heads,),
-        in_specs=[whole(8, tokens + steps), whole(tokens + steps, 8), column(0),
-                  column(0), column(heads), column(0), column(heads)],
-        out_specs=[whole(total, steps), whole(tokens, width), whole(width, width),
-                   whole(tokens, width), whole(width, width)],
+        grid=(groups,),
+        in_specs=[whole(8, tokens), columns(0), columns(0), columns(groups), columns(0), columns(groups)],
+        out_specs=[several(total, steps), several(tokens, width), several(width, width),
+                   several(tokens, width), several(width, width)],
         out_shape=[jax.ShapeDtypeStruct((heads, total, steps), BF16),
                    jax.ShapeDtypeStruct((heads, tokens, width), BF16),
                    jax.ShapeDtypeStruct((heads, width, width), F32),
@@ -360,7 +385,7 @@
         compiler_params=pltpu.CompilerParams(vmem_limit_bytes=48 << 20),
         cost_estimate=pl.CostEstimate(flops=8 << 30, bytes_accessed=8 << 20, transcendentals=0),
         name="local",
-    )(rows, cols, queries, keys2, keys2, values2, values2)
+    )(rows, queries, keys2, keys2, values2, values2)
 
     up, d = pl.pallas_call(
         adjoint_kernel,
@@ -391,12 +416,12 @@
 
     sections = lax.axis_size("section")
     features = out_weight.shape[1] // (2 * sections)
-    flat = jax.ShapeDtypeStruct((tokens, heads * width), F32)
-    output, g0, g1 = pl.pallas_call(
+    output, value_grads = pl.pallas_call(
         functools.partial(output_kernel, sections),
         in_specs=[vmem] * 7,
-        out_specs=[vmem] * 3,
-        out_shape=[jax.ShapeDtypeStruct((features, tokens), BF16), flat, flat],
+        out_specs=[vmem] * 2,
+        out_shape=[jax.ShapeDtypeStruct((features, tokens), BF16),
+                   jax.ShapeDtypeStruct((tokens, 2, heads * width), F32)],
         scratch_shapes=[pltpu.VMEM((heads * width, tokens), BF16),
                         pltpu.VMEM((sections, features, tokens), F32),
                         pltpu.VMEM((sections, features, tokens), F32),
@@ -407,7 +432,7 @@
             collective_id=1, has_side_effects=True, vmem_limit_bytes=48 << 20),
         name="output",
     )(r, o, state, y, up, adjoint, out_weight)
-    return output, jnp.stack([g0, g1], axis=1)
+    return output, value_grads
 
 
 def solution(mesh):

time: 82.9 us -> 72.9 us (0.88)
  Pallas kernels: 57.9 us -> 45 us
  local copies, waits for them, and re-layouts: 8.34 us -> 12 us
    pallas_call x1, Pallas kernels: 28.1 us -> 15.2 us  [per_device(): pl.pallas_call(local_kernel, grid=(groups,), in_specs=[whole(8, tokens),...]
    unnamed x19 -> x24, local copies, waits for them, and re-layouts: 6.81 us -> 10.5 us
  transfers between devices with their start and end apart: 1 -> 1, of which waited for: 0 -> 0; matrix products, arithmetic and copies ran while one was open for 4% -> 7% of each run, Pallas kernels for 34% -> 21%
where the time goes in v2:
time: 72.9 us; the launch traced here: 72.4 us
  Pallas kernels  45 us (62%)
  between operations  14.1 us (19%)
  local copies, waits for them, and re-layouts  12 us (16%)
    pallas_call x1, Pallas kernels, per_device(): pl.pallas_call(local_kernel, grid=(groups,), in_specs=[whole(8, tokens),...  15.2 us
    pallas_call x1, Pallas kernels, per_device(): pl.pallas_call(functools.partial(chain_kernel, devices), in_specs=[vmem]...  14.4 us
    pallas_call x1, Pallas kernels, per_device(): pl.pallas_call(functools.partial(output_kernel, sections), in_specs=[vmem...  12.9 us
    unnamed x24, local copies, waits for them, and re-layouts  10.5 us
    pallas_call x1, Pallas kernels, per_device(): pl.pallas_call(adjoint_kernel, grid=(heads,), in_specs=[pl.BlockSpec(cot....  2.47 us
  transfers between devices with their start and end apart: 1, of which 0 were waited for; matrix products, arithmetic and copies ran while one was open for 7% of the time, Pallas kernels for 21%

profile of v2, /device:TPU:0, one launch (start us, length us, event | category | flops | bytes accessed | tf_op | source)
XLA Modules:
  0.0 72.4 jit_solution(14173135364123180497)
XLA Ops:
  7.2 0.0 all-gather.2.cloned.1.call-start
  7.2 0.7 all-gather.2.cloned.1.call-update
  7.9 0.7 fusion
  8.6 0.7 reshape.21
  9.3 0.7 convert_element_type.3
  10.0 1.1 %copy.10 = bf16[32,8,2,512]{3,1,2,0:T(8,128)(2,1)S(1)} copy(bf16[32,8,2,512]{3,2,1,0:T(2,128)(2,1)} %bitcast.10) | data formatting | bytes 1048576
  11.1 1.9 %copy.11 = bf16[32,8,2,512]{3,1,2,0:T(8,128)(2,1)} copy(bf16[32,8,2,512]{3,2,1,0:T(2,128)(2,1)} %bitcast.11) | data formatting | bytes 1048576
  13.1 0.0 copy-start.4
  13.1 1.0 %copy-done.4 = bf16[32,8,2,512]{3,1,2,0:T(8,128)(2,1)S(1)} copy-done((bf16[32,8,2,512]{3,1,2,0:T(8,128)(2,1)S(1)}, bf16[32,8,2,512]{3,1,2,0:T(8,128)(2,1)}, u32[]{:S(2)}) %copy-start.4) | copy-done | bytes 524312
  14.1 0.0 copy-start.9
  14.1 0.9 %copy-done.9 = bf16[256,512]{1,0:T(8,128)(2,1)S(1)} copy-done((bf16[256,512]{1,0:T(8,128)(2,1)S(1)}, bf16[256,512]{1,0:T(8,128)(2,1)}, u32[]{:S(2)}) %copy-start.9) | copy-done | bytes 262168
  15.1 0.0 copy-start
  15.1 15.2 %local.1 = (bf16[4,384,512]{2,1,0:T(8,128)(2,1)S(1)}, bf16[4,256,128]{2,1,0:T(8,128)(2,1)S(1)}, f32[4,128,128]{2,1,0:T(8,128)S(1)}, f32[4,256,128]{2,1,0:T(8,128)S(1)}, f32[4,128,128]{2,1,0:T(8,128)S(1)}) custom-call(f32[2,8,256]{2,1,0:T(8,128)S(1)} %concatenate.3.rows_ref, bf16[256,512]{1,0:T(8,128)(2,1)S(1)} %copy-done.9, bf16[256,1024]{1,0:T(8,128)(2,1)S(1)} %bitcast.6, ...), custom_call_target="tpu_custom_call" | custom-call | flops 8589934592 | bytes 8388608 | tf_op jit(solution)/shard_map/local/pallas_call | solution.py:374
  30.2 0.0 copy-start.1
  30.2 1.2 %copy-done.1 = bf16[4,384,512]{2,1,0:T(8,128)(2,1)} copy-done((bf16[4,384,512]{2,1,0:T(8,128)(2,1)}, bf16[4,384,512]{2,1,0:T(8,128)(2,1)S(1)}, u32[]{:S(2)}) %copy-start.1) | copy-done | bytes 1572888
  31.4 0.0 copy-start.5
  31.4 0.7 copy-done.5
  32.1 0.0 copy-start.7
  32.1 0.7 copy-done.7
  32.8 0.0 all-gather.2.cloned.1.call-done.cot_ref
  32.8 0.0 copy-done
  32.8 0.0 copy-start.3
  32.8 1.2 %copy-done.3 = bf16[256,2048]{1,0:T(8,128)(2,1)S(1)} copy-done((bf16[256,2048]{1,0:T(8,128)(2,1)S(1)}, bf16[256,2048]{1,0:T(8,128)(2,1)}, u32[]{:S(2)}) %copy-start.3) | copy-done | bytes 1048600
  34.0 0.0 copy-start.6
  34.0 0.0 copy-start.8
  34.0 0.0 copy-start.2
  34.0 2.5 %adjoint.1 = (bf16[4,256,128]{2,1,0:T(8,128)(2,1)S(1)}, f32[4,128,128]{2,1,0:T(8,128)S(1)}) custom-call(bf16[256,2048]{1,0:T(8,128)(2,1)S(1)} %copy-done.3, bf16[512,2048]{1,0:T(8,128)(2,1)S(1)} %copy-done, bf16[4,256,128]{2,1,0:T(8,128)(2,1)S(1)} %get-tuple-element.11.r_ref), custom_call_target="tpu_custom_call" | custom-call | tf_op jit(solution)/shard_map/adjoint/pallas_call | solution.py:390
  36.5 0.0 copy-done.6
  36.5 0.0 copy-done.8
  36.5 14.4 %chain.1 = (bf16[4,128,128]{2,1,0:T(8,128)(2,1)S(1)}, bf16[4,128,128]{2,1,0:T(8,128)(2,1)S(1)}) custom-call(f32[4,128,128]{2,1,0:T(8,128)S(1)} %copy-done.6, f32[4,128,128]{2,1,0:T(8,128)S(1)} %copy-done.8, f32[4,128,128]{2,1,0:T(8,128)S(1)} %get-tuple-element.15.d_ref), custom_call_target="tpu_custom_call" | custom-call | tf_op jit(solution)/shard_map/chain/pallas_call | solution.py:406
  51.0 0.0 copy-done.2
  51.0 12.9 %output.1 = (bf16[512,256]{1,0:T(8,128)(2,1)S(1)}, f32[256,2,512]{2,1,0:T(2,128)S(1)}) custom-call(bf16[4,256,128]{2,1,0:T(8,128)(2,1)S(1)} %get-tuple-element.11.r_ref, f32[4,256,128]{2,1,0:T(8,128)S(1)} %get-tuple-element.12.o_ref, bf16[4,128,128]{2,1,0:T(8,128)(2,1)S(1)} %get-tuple-element.16.s_ref, bf16[4,384,512]{2,1,0:T(8,128)(2,1)S(1)} %copy-done.2, ...), custom_call_target="tpu_custom_call" | custom-call | tf_op jit(solution)/shard_map/output/pallas_call | solution.py:419
  63.9 0.7 copy.14
  64.6 1.0 %copy.15 = f32[256,2,512]{2,1,0:T(2,128)} copy(f32[256,2,512]{2,1,0:T(2,128)S(1)} %get-tuple-element.25) | data formatting | bytes 2097152
  (5 shorter events, 0.1 us)
Async XLA Ops:
  7.2 25.6 %all-gather.2.cloned.1.call-start = ((), (), s32[]{:S(2)}) async-start(), calls=%async_computation | async-start | bytes 1310720 | tf_op jit(solution)/shard_map/all_gather | solution.py:352
  13.1 1.0 %copy-start.4 = (bf16[32,8,2,512]{3,1,2,0:T(8,128)(2,1)S(1)}, bf16[32,8,2,512]{3,1,2,0:T(8,128)(2,1)}, u32[]{:S(2)}) copy-start(bf16[32,8,2,512]{3,1,2,0:T(8,128)(2,1)} %copy.11) | copy-start | bytes 1572868
  14.1 0.9 %copy-start.9 = (bf16[256,512]{1,0:T(8,128)(2,1)S(1)}, bf16[256,512]{1,0:T(8,128)(2,1)}, u32[]{:S(2)}) copy-start(bf16[256,512]{1,0:T(8,128)(2,1)} %q_ref.1) | copy-start | bytes 786436
  15.1 17.7 %copy-start = (bf16[512,2048]{1,0:T(8,128)(2,1)S(1)}, bf16[512,2048]{1,0:T(8,128)(2,1)}, u32[]{:S(2)}) copy-start(bf16[512,2048]{1,0:T(8,128)(2,1)} %w_ref.3) | copy-start | bytes 6291460
  30.2 1.2 %copy-start.1 = (bf16[4,384,512]{2,1,0:T(8,128)(2,1)}, bf16[4,384,512]{2,1,0:T(8,128)(2,1)S(1)}, u32[]{:S(2)}) copy-start(bf16[4,384,512]{2,1,0:T(8,128)(2,1)S(1)} %get-tuple-element.17.y_ref) | copy-start | bytes 4718596
  31.4 0.7 copy-start.5
  32.1 0.7 copy-start.7
  32.8 1.2 %copy-start.3 = (bf16[256,2048]{1,0:T(8,128)(2,1)S(1)}, bf16[256,2048]{1,0:T(8,128)(2,1)}, u32[]{:S(2)}) copy-start(bf16[256,2048]{1,0:T(8,128)(2,1)} %all-gather.2.cloned.1.call-done.cot_ref) | copy-start | bytes 3145732
  34.0 2.5 %copy-start.6 = (f32[4,128,128]{2,1,0:T(8,128)S(1)}, f32[4,128,128]{2,1,0:T(8,128)}, u32[]{:S(2)}) copy-start(f32[4,128,128]{2,1,0:T(8,128)} %copy-done.5) | copy-start | bytes 786436
  34.0 2.5 %copy-start.8 = (f32[4,128,128]{2,1,0:T(8,128)S(1)}, f32[4,128,128]{2,1,0:T(8,128)}, u32[]{:S(2)}) copy-start(f32[4,128,128]{2,1,0:T(8,128)} %copy-done.7) | copy-start | bytes 786436
  34.0 16.9 %copy-start.2 = (bf16[4,384,512]{2,1,0:T(8,128)(2,1)S(1)}, bf16[4,384,512]{2,1,0:T(8,128)(2,1)}, u32[]{:S(2)}) copy-start(bf16[4,384,512]{2,1,0:T(8,128)(2,1)} %copy-done.1) | copy-start | bytes 4718596
Sparse Core Ops, SparseCore 0:
  9.6 19.4 all-gather.1

commit v3 on v2

--- a/solution.py
+++ b/solution.py
@@ -178,20 +178,24 @@
         m_ref[g] = jnp.where(iota((width, width), 0) == iota((width, width), 1), gamma_end, 0.0) - moved[tokens:]
 
 
-def adjoint_kernel(cot_ref, w_ref, r_ref, up_ref, d_ref):
-    up = dot1(cot_ref[...], w_ref[...], NT).astype(BF16)
-    up_ref[0] = up
-    d_ref[0] = dot1(r_ref[0], up, TN)
-
-
 MESH = pl.DeviceIdType.MESH
 
 
-def chain_kernel(devices, m_ref, b_ref, d_ref, s_ref, ds_ref, s_in, s_out, ds_in, ds_out,
-                 s_sent, s_got, ds_sent, ds_got):
-    heads = m_ref.shape[0]
+def tail_kernel(devices, sections, m_ref, b_ref, r_ref, o_ref, y_ref, cot_ref, w_ref,
+                out_ref, g_ref,
+                s_in, s_out, ds_in, ds_out, d, up_, mh, ml,
+                mixed, pair_out, pair_in, cross_out, cross_in,
+                s_sent, s_got, ds_sent, ds_got, pair_sent, pair_got, cross_sent, cross_got):
+    heads, tokens, width = r_ref.shape
+    features = out_ref.shape[0]
     place = lax.axis_index("seq")
+    section, core = lax.axis_index("section"), lax.axis_index("head")
+    sibling = 1 - core
     first, last = place == 0, place == devices - 1
+
+    def peer(k):
+        return lax.rem(section + k, sections)
+
     barrier = pltpu.get_barrier_semaphore()
 
     @pl.when(jnp.logical_not(first))
@@ -202,8 +206,12 @@
     def _():
         pl.semaphore_signal(barrier, inc=1, device_id={"seq": place + 1}, device_id_type=MESH)
 
-    if devices > 1:
-        pl.semaphore_wait(barrier, jnp.where(first | last, 1, 2))
+    pl.semaphore_signal(barrier, inc=1, device_id={"head": sibling}, device_id_type=MESH)
+    for k in range(1, sections):
+        pl.semaphore_signal(barrier, inc=1, device_id={"section": peer(k)}, device_id_type=MESH)
+    for h in range(heads):
+        mh[h], ml[h] = halves(m_ref[h])
+    pl.semaphore_wait(barrier, sections + jnp.where(first, 0, 1) + jnp.where(last, 0, 1))
 
     def up(h):
         return pltpu.make_async_remote_copy(
@@ -227,12 +235,9 @@
 
             @pl.when(jnp.logical_not(last))
             def _():
-                mh, ml = halves(m_ref[h])
                 s = s_in[h]
-                s_out[h] = (dot1(mh, s) + dot1(ml, s) + b_ref[h]).astype(BF16)
+                s_out[h] = (dot1(mh[h], s) + dot1(ml[h], s) + b_ref[h]).astype(BF16)
                 up(h).start()
-
-            s_ref[h] = s_in[h]
 
     def backward():
         for h in range(heads):
@@ -246,18 +251,23 @@
 
             @pl.when(jnp.logical_not(first))
             def _():
-                mh, ml = halves(m_ref[h])
                 ds = ds_in[h]
-                ds_out[h] = (dot1(mh, ds, TN) + dot1(ml, ds, TN) + d_ref[h]).astype(BF16)
+                ds_out[h] = (dot1(mh[h], ds, TN) + dot1(ml[h], ds, TN) + d[h]).astype(BF16)
                 down(h).start()
 
-            ds_ref[h] = ds_in[h]
-
     low = 2 * place < devices
 
     @pl.when(low)
     def _():
         forward()
+
+    for h in range(heads):
+        upstream = dot1(cot_ref[...], w_ref[h * width:(h + 1) * width, :], NT).astype(BF16)
+        up_[h] = upstream
+        d[h] = dot1(r_ref[h], upstream, TN)
+
+    @pl.when(low)
+    def _():
         backward()
 
     @pl.when(jnp.logical_not(low))
@@ -265,37 +275,8 @@
         backward()
         forward()
 
-    @pl.when(jnp.logical_not(last))
-    def _():
-        for h in range(heads):
-            up(h).wait_send()
-
-    @pl.when(jnp.logical_not(first))
-    def _():
-        for h in range(heads):
-            down(h).wait_send()
-
-
-def output_kernel(sections, r_ref, o_ref, s_ref, y_ref, up_ref, ds_ref, w_ref,
-                  out_ref, g_ref,
-                  mixed, pair_out, pair_in, cross_out, cross_in,
-                  pair_sent, pair_got, cross_sent, cross_got):
-    heads, tokens, width = r_ref.shape
-    features = out_ref.shape[0]
-    section, core = lax.axis_index("section"), lax.axis_index("head")
-    sibling = 1 - core
-
-    def peer(k):
-        return lax.rem(section + k, sections)
-
-    barrier = pltpu.get_barrier_semaphore()
-    pl.semaphore_signal(barrier, inc=1, device_id={"head": sibling}, device_id_type=MESH)
-    for k in range(1, sections):
-        pl.semaphore_signal(barrier, inc=1, device_id={"section": peer(k)}, device_id_type=MESH)
-
     for h in range(heads):
-        mixed[h * width:(h + 1) * width, :] = (dot1(r_ref[h], s_ref[h]) + o_ref[h]).T.astype(BF16)
-    pl.semaphore_wait(barrier, sections)
+        mixed[h * width:(h + 1) * width, :] = (dot1(r_ref[h], s_in[h]) + o_ref[h]).T.astype(BF16)
 
     def partial(target, side):
         start = pl.multiple_of((target * 2 + side) * features, 128)
@@ -312,7 +293,7 @@
             recv_sem=cross_got.at[k - 1], device_id={"section": peer(k)}, device_id_type=MESH)
 
     order = list(range(1, sections)) + [0]
-    for k in order:
+    for k in range(1, sections):
         pair_out[k] = partial(peer(k), sibling)
         pair(k).start()
     for k in range(1, sections):
@@ -320,8 +301,10 @@
         pair(k).wait_recv()
         cross_out[k - 1] = (mine + pair_in[k]).astype(BF16)
         cross(k).start()
+    pair_out[0] = partial(section, sibling)
+    pair(0).start()
     for h in range(heads):
-        right = jnp.concatenate([up_ref[h], ds_ref[h]], axis=0)
+        right = jnp.concatenate([up_[h], ds_in[h]], axis=0)
         grad = dot1(y_ref[h], right, TN)
         lanes = slice(h * width, (h + 1) * width)
         for b in range(tokens // HALF):
@@ -340,6 +323,16 @@
     for k in range(1, sections):
         cross(k).wait_send()
 
+    @pl.when(jnp.logical_not(last))
+    def _():
+        for h in range(heads):
+            up(h).wait_send()
+
+    @pl.when(jnp.logical_not(first))
+    def _():
+        for h in range(heads):
+            down(h).wait_send()
+
 
 def per_device(queries, reflect_keys, reflect_values, reflect_betas, decay_rates, resets,
                out_weight, out_cotangent):
@@ -382,56 +375,35 @@
                    jax.ShapeDtypeStruct((heads, width, width), F32),
                    jax.ShapeDtypeStruct((heads, tokens, width), F32),
                    jax.ShapeDtypeStruct((heads, width, width), F32)],
-        compiler_params=pltpu.CompilerParams(vmem_limit_bytes=48 << 20),
+        compiler_params=pltpu.CompilerParams(vmem_limit_bytes=28 << 20),
         cost_estimate=pl.CostEstimate(flops=8 << 30, bytes_accessed=8 << 20, transcendentals=0),
         name="local",
     )(rows, queries, keys2, keys2, values2, values2)
 
-    up, d = pl.pallas_call(
-        adjoint_kernel,
-        grid=(heads,),
-        in_specs=[pl.BlockSpec(cot.shape, lambda h: (0, 0)),
-                  pl.BlockSpec((width, out_weight.shape[1]), lambda h: (h, 0)),
-                  whole(tokens, width)],
-        out_specs=[whole(tokens, width), whole(width, width)],
-        out_shape=[jax.ShapeDtypeStruct((heads, tokens, width), BF16),
-                   jax.ShapeDtypeStruct((heads, width, width), F32)],
-        compiler_params=pltpu.CompilerParams(vmem_limit_bytes=32 << 20),
-        name="adjoint",
-    )(cot, out_weight, r)
-
     square = (heads, width, width)
     vmem = pl.BlockSpec(memory_space=pltpu.VMEM)
     dma = pltpu.SemaphoreType.DMA
-    state, adjoint = pl.pallas_call(
-        functools.partial(chain_kernel, devices),
-        in_specs=[vmem] * 3,
-        out_specs=[vmem] * 2,
-        out_shape=[jax.ShapeDtypeStruct(square, BF16)] * 2,
-        scratch_shapes=[pltpu.VMEM(square, BF16)] * 4 + [dma((heads,))] * 4,
-        compiler_params=pltpu.CompilerParams(
-            collective_id=0, has_side_effects=True, vmem_limit_bytes=32 << 20),
-        name="chain",
-    )(m, b, d)
-
     sections = lax.axis_size("section")
     features = out_weight.shape[1] // (2 * sections)
     output, value_grads = pl.pallas_call(
-        functools.partial(output_kernel, sections),
+        functools.partial(tail_kernel, devices, sections),
         in_specs=[vmem] * 7,
         out_specs=[vmem] * 2,
         out_shape=[jax.ShapeDtypeStruct((features, tokens), BF16),
                    jax.ShapeDtypeStruct((tokens, 2, heads * width), F32)],
-        scratch_shapes=[pltpu.VMEM((heads * width, tokens), BF16),
-                        pltpu.VMEM((sections, features, tokens), F32),
-                        pltpu.VMEM((sections, features, tokens), F32),
-                        pltpu.VMEM((sections - 1, features, tokens), BF16),
-                        pltpu.VMEM((sections - 1, features, tokens), BF16),
-                        dma((sections,)), dma((sections,)), dma((sections - 1,)), dma((sections - 1,))],
+        scratch_shapes=[pltpu.VMEM(square, BF16)] * 4
+        + [pltpu.VMEM(square, F32), pltpu.VMEM((heads, tokens, width), BF16)]
+        + [pltpu.VMEM(square, BF16)] * 2
+        + [pltpu.VMEM((heads * width, tokens), BF16),
+           pltpu.VMEM((sections, features, tokens), F32),
+           pltpu.VMEM((sections, features, tokens), F32),
+           pltpu.VMEM((sections - 1, features, tokens), BF16),
+           pltpu.VMEM((sections - 1, features, tokens), BF16)]
+        + [dma((heads,))] * 4 + [dma((sections,))] * 2 + [dma((sections - 1,))] * 2,
         compiler_params=pltpu.CompilerParams(
-            collective_id=1, has_side_effects=True, vmem_limit_bytes=48 << 20),
-        name="output",
-    )(r, o, state, y, up, adjoint, out_weight)
+            collective_id=0, has_side_effects=True, vmem_limit_bytes=24 << 20),
+        name="tail",
+    )(m, b, r, o, y, cot, out_weight)
     return output, value_grads
 
 

time: 72.9 us -> 73.2 us (level)
  Pallas kernels: 45 us -> 41.4 us
  local copies, waits for them, and re-layouts: 12 us -> 15.2 us
    pallas_call x3 -> x1, Pallas kernels: 29.8 us -> 26.3 us  [per_device(): pl.pallas_call(functools.partial(tail_kernel, devices, sections), in_spec...]
    unnamed x24, local copies, waits for them, and re-layouts: 10.5 us -> 13.8 us
where the time goes in v3:
time: 73.2 us; the launch traced here: 72.2 us
  Pallas kernels  41.4 us (57%)
  local copies, waits for them, and re-layouts  15.2 us (21%)
  between operations  14.1 us (19%)
    pallas_call x1, Pallas kernels, per_device(): pl.pallas_call(functools.partial(tail_kernel, devices, sections), in_spec...  26.3 us
    pallas_call x1, Pallas kernels, per_device(): pl.pallas_call(local_kernel, grid=(groups,), in_specs=[whole(8, tokens),...  15.2 us
    unnamed x24, local copies, waits for them, and re-layouts  13.8 us
  transfers between devices with their start and end apart: 1, of which 0 were waited for; matrix products, arithmetic and copies ran while one was open for 7% of the time, Pallas kernels for 21%

profile of v3, /device:TPU:0, one launch (start us, length us, event | category | flops | bytes accessed | tf_op | source)
XLA Modules:
  0.0 72.2 jit_solution(6438328197329578506)
XLA Ops:
  7.2 0.0 all-gather.2.cloned.1.call-start
  7.2 0.7 all-gather.2.cloned.1.call-update
  7.9 0.7 convert_element_type.3
  8.6 0.7 reshape.21
  9.3 0.7 fusion
  10.0 1.1 %copy.10 = bf16[32,8,2,512]{3,1,2,0:T(8,128)(2,1)S(1)} copy(bf16[32,8,2,512]{3,2,1,0:T(2,128)(2,1)} %bitcast.10) | data formatting | bytes 1048576
  11.1 1.9 %copy.11 = bf16[32,8,2,512]{3,1,2,0:T(8,128)(2,1)} copy(bf16[32,8,2,512]{3,2,1,0:T(2,128)(2,1)} %bitcast.11) | data formatting | bytes 1048576
  13.1 0.0 copy-start.4
  13.1 1.0 %copy-done.4 = bf16[32,8,2,512]{3,1,2,0:T(8,128)(2,1)S(1)} copy-done((bf16[32,8,2,512]{3,1,2,0:T(8,128)(2,1)S(1)}, bf16[32,8,2,512]{3,1,2,0:T(8,128)(2,1)}, u32[]{:S(2)}) %copy-start.4) | copy-done | bytes 524312
  14.1 0.0 copy-start.9
  14.1 0.9 %copy-done.9 = bf16[256,512]{1,0:T(8,128)(2,1)S(1)} copy-done((bf16[256,512]{1,0:T(8,128)(2,1)S(1)}, bf16[256,512]{1,0:T(8,128)(2,1)}, u32[]{:S(2)}) %copy-start.9) | copy-done | bytes 262168
  15.1 0.0 copy-start
  15.1 15.2 %local.1 = (bf16[4,384,512]{2,1,0:T(8,128)(2,1)S(1)}, bf16[4,256,128]{2,1,0:T(8,128)(2,1)S(1)}, f32[4,128,128]{2,1,0:T(8,128)S(1)}, f32[4,256,128]{2,1,0:T(8,128)S(1)}, f32[4,128,128]{2,1,0:T(8,128)S(1)}) custom-call(f32[2,8,256]{2,1,0:T(8,128)S(1)} %concatenate.3.rows_ref, bf16[256,512]{1,0:T(8,128)(2,1)S(1)} %copy-done.9, bf16[256,1024]{1,0:T(8,128)(2,1)S(1)} %bitcast.6, ...), custom_call_target="tpu_custom_call" | custom-call | flops 8589934592 | bytes 8388608 | tf_op jit(solution)/shard_map/local/pallas_call | solution.py:367
  30.2 0.0 copy-start.1
  30.2 1.2 %copy-done.1 = bf16[4,384,512]{2,1,0:T(8,128)(2,1)} copy-done((bf16[4,384,512]{2,1,0:T(8,128)(2,1)}, bf16[4,384,512]{2,1,0:T(8,128)(2,1)S(1)}, u32[]{:S(2)}) %copy-start.1) | copy-done | bytes 1572888
  31.4 0.0 copy-start.5
  31.4 0.7 copy-done.5
  32.1 0.0 copy-start.7
  32.1 0.7 copy-done.7
  32.8 0.0 all-gather.2.cloned.1.call-done.cot_ref
  32.8 0.0 copy-done
  32.8 0.0 copy-start.2
  32.8 1.4 %copy-done.2 = bf16[4,384,512]{2,1,0:T(8,128)(2,1)S(1)} copy-done((bf16[4,384,512]{2,1,0:T(8,128)(2,1)S(1)}, bf16[4,384,512]{2,1,0:T(8,128)(2,1)}, u32[]{:S(2)}) %copy-start.2) | copy-done | bytes 1572888
  34.2 0.0 copy-start.3
  34.2 1.2 %copy-done.3 = bf16[256,2048]{1,0:T(8,128)(2,1)S(1)} copy-done((bf16[256,2048]{1,0:T(8,128)(2,1)S(1)}, bf16[256,2048]{1,0:T(8,128)(2,1)}, u32[]{:S(2)}) %copy-start.3) | copy-done | bytes 1048600
  35.4 0.0 copy-start.6
  35.4 0.9 %copy-done.6 = f32[4,128,128]{2,1,0:T(8,128)S(1)} copy-done((f32[4,128,128]{2,1,0:T(8,128)S(1)}, f32[4,128,128]{2,1,0:T(8,128)}, u32[]{:S(2)}) %copy-start.6) | copy-done | bytes 262168
  36.4 0.0 copy-start.8
  36.4 0.9 %copy-done.8 = f32[4,128,128]{2,1,0:T(8,128)S(1)} copy-done((f32[4,128,128]{2,1,0:T(8,128)S(1)}, f32[4,128,128]{2,1,0:T(8,128)}, u32[]{:S(2)}) %copy-start.8) | copy-done | bytes 262168
  37.3 26.3 %tail.1 = (bf16[512,256]{1,0:T(8,128)(2,1)S(1)}, f32[256,2,512]{2,1,0:T(2,128)S(1)}) custom-call(f32[4,128,128]{2,1,0:T(8,128)S(1)} %copy-done.6, f32[4,128,128]{2,1,0:T(8,128)S(1)} %copy-done.8, bf16[4,256,128]{2,1,0:T(8,128)(2,1)S(1)} %get-tuple-element.9.r_ref, f32[4,256,128]{2,1,0:T(8,128)S(1)} %get-tuple-element.10.o_ref, ...), custom_call_target="tpu_custom_call" | custom-call | tf_op jit(solution)/shard_map/tail/pallas_call | solution.py:388
  63.6 0.7 copy.14
  64.3 1.0 %copy.15 = f32[256,2,512]{2,1,0:T(2,128)} copy(f32[256,2,512]{2,1,0:T(2,128)S(1)} %get-tuple-element.17) | data formatting | bytes 2097152
  (5 shorter events, 0.1 us)
Async XLA Ops:
  7.2 25.6 %all-gather.2.cloned.1.call-start = ((), (), s32[]{:S(2)}) async-start(), calls=%async_computation | async-start | bytes 1310720 | tf_op jit(solution)/shard_map/all_gather | solution.py:345
  13.1 1.0 %copy-start.4 = (bf16[32,8,2,512]{3,1,2,0:T(8,128)(2,1)S(1)}, bf16[32,8,2,512]{3,1,2,0:T(8,128)(2,1)}, u32[]{:S(2)}) copy-start(bf16[32,8,2,512]{3,1,2,0:T(8,128)(2,1)} %copy.11) | copy-start | bytes 1572868
  14.1 0.9 %copy-start.9 = (bf16[256,512]{1,0:T(8,128)(2,1)S(1)}, bf16[256,512]{1,0:T(8,128)(2,1)}, u32[]{:S(2)}) copy-start(bf16[256,512]{1,0:T(8,128)(2,1)} %q_ref.1) | copy-start | bytes 786436
  15.1 17.7 %copy-start = (bf16[512,2048]{1,0:T(8,128)(2,1)S(1)}, bf16[512,2048]{1,0:T(8,128)(2,1)}, u32[]{:S(2)}) copy-start(bf16[512,2048]{1,0:T(8,128)(2,1)} %w_ref.1) | copy-start | bytes 6291460
  30.2 1.2 %copy-start.1 = (bf16[4,384,512]{2,1,0:T(8,128)(2,1)}, bf16[4,384,512]{2,1,0:T(8,128)(2,1)S(1)}, u32[]{:S(2)}) copy-start(bf16[4,384,512]{2,1,0:T(8,128)(2,1)S(1)} %get-tuple-element.11.y_ref) | copy-start | bytes 4718596
  31.4 0.7 copy-start.5
  32.1 0.7 copy-start.7
  32.8 1.4 %copy-start.2 = (bf16[4,384,512]{2,1,0:T(8,128)(2,1)S(1)}, bf16[4,384,512]{2,1,0:T(8,128)(2,1)}, u32[]{:S(2)}) copy-start(bf16[4,384,512]{2,1,0:T(8,128)(2,1)} %copy-done.1) | copy-start | bytes 4718596
  34.2 1.2 %copy-start.3 = (bf16[256,2048]{1,0:T(8,128)(2,1)S(1)}, bf16[256,2048]{1,0:T(8,128)(2,1)}, u32[]{:S(2)}) copy-start(bf16[256,2048]{1,0:T(8,128)(2,1)} %all-gather.2.cloned.1.call-done.cot_ref) | copy-start | bytes 3145732
  35.4 0.9 %copy-start.6 = (f32[4,128,128]{2,1,0:T(8,128)S(1)}, f32[4,128,128]{2,1,0:T(8,128)}, u32[]{:S(2)}) copy-start(f32[4,128,128]{2,1,0:T(8,128)} %copy-done.5) | copy-start | bytes 786436
  36.4 0.9 %copy-start.8 = (f32[4,128,128]{2,1,0:T(8,128)S(1)}, f32[4,128,128]{2,1,0:T(8,128)}, u32[]{:S(2)}) copy-start(f32[4,128,128]{2,1,0:T(8,128)} %copy-done.7) | copy-start | bytes 786436
Sparse Core Ops, SparseCore 0:
  9.6 19.4 all-gather.1

commit v4 on v3

--- a/solution.py
+++ b/solution.py
@@ -181,13 +181,19 @@
 MESH = pl.DeviceIdType.MESH
 
 
-def tail_kernel(devices, sections, m_ref, b_ref, r_ref, o_ref, y_ref, cot_ref, w_ref,
+def tail_kernel(devices, sections, m_hbm, b_hbm, r_hbm, o_hbm, y_hbm, cot_hbm, w_hbm,
                 out_ref, g_ref,
+                m_ref, b_ref, r_ref, o_ref, y_ref, cot_ref, w_ref, loaded,
                 s_in, s_out, ds_in, ds_out, d, up_, mh, ml,
                 mixed, pair_out, pair_in, cross_out, cross_in,
                 s_sent, s_got, ds_sent, ds_got, pair_sent, pair_got, cross_sent, cross_got):
     heads, tokens, width = r_ref.shape
     features = out_ref.shape[0]
+    pairs = ((m_hbm, m_ref), (b_hbm, b_ref), (cot_hbm, cot_ref), (w_hbm, w_ref), (r_hbm, r_ref),
+             (o_hbm, o_ref), (y_hbm, y_ref))
+    loads = [pltpu.make_async_copy(a, c, loaded.at[i]) for i, (a, c) in enumerate(pairs)]
+    for load in loads:
+        load.start()
     place = lax.axis_index("seq")
     section, core = lax.axis_index("section"), lax.axis_index("head")
     sibling = 1 - core
@@ -209,6 +215,8 @@
     pl.semaphore_signal(barrier, inc=1, device_id={"head": sibling}, device_id_type=MESH)
     for k in range(1, sections):
         pl.semaphore_signal(barrier, inc=1, device_id={"section": peer(k)}, device_id_type=MESH)
+    loads[0].wait()
+    loads[1].wait()
     for h in range(heads):
         mh[h], ml[h] = halves(m_ref[h])
     pl.semaphore_wait(barrier, sections + jnp.where(first, 0, 1) + jnp.where(last, 0, 1))
@@ -261,6 +269,8 @@
     def _():
         forward()
 
+    for i in (2, 3, 4):
+        loads[i].wait()
     for h in range(heads):
         upstream = dot1(cot_ref[...], w_ref[h * width:(h + 1) * width, :], NT).astype(BF16)
         up_[h] = upstream
@@ -275,6 +285,7 @@
         backward()
         forward()
 
+    loads[5].wait()
     for h in range(heads):
         mixed[h * width:(h + 1) * width, :] = (dot1(r_ref[h], s_in[h]) + o_ref[h]).T.astype(BF16)
 
@@ -303,6 +314,7 @@
         cross(k).start()
     pair_out[0] = partial(section, sibling)
     pair(0).start()
+    loads[6].wait()
     for h in range(heads):
         right = jnp.concatenate([up_[h], ds_in[h]], axis=0)
         grad = dot1(y_ref[h], right, TN)
@@ -375,7 +387,7 @@
                    jax.ShapeDtypeStruct((heads, width, width), F32),
                    jax.ShapeDtypeStruct((heads, tokens, width), F32),
                    jax.ShapeDtypeStruct((heads, width, width), F32)],
-        compiler_params=pltpu.CompilerParams(vmem_limit_bytes=28 << 20),
+        compiler_params=pltpu.CompilerParams(vmem_limit_bytes=58 << 20),
         cost_estimate=pl.CostEstimate(flops=8 << 30, bytes_accessed=8 << 20, transcendentals=0),
         name="local",
     )(rows, queries, keys2, keys2, values2, values2)
@@ -387,11 +399,12 @@
     features = out_weight.shape[1] // (2 * sections)
     output, value_grads = pl.pallas_call(
         functools.partial(tail_kernel, devices, sections),
-        in_specs=[vmem] * 7,
+        in_specs=[pl.BlockSpec(memory_space=pl.ANY)] * 7,
         out_specs=[vmem] * 2,
         out_shape=[jax.ShapeDtypeStruct((features, tokens), BF16),
                    jax.ShapeDtypeStruct((tokens, 2, heads * width), F32)],
-        scratch_shapes=[pltpu.VMEM(square, BF16)] * 4
+        scratch_shapes=[pltpu.VMEM(a.shape, a.dtype) for a in (m, b, r, o, y, cot, out_weight)]
+        + [dma((7,))] + [pltpu.VMEM(square, BF16)] * 4
         + [pltpu.VMEM(square, F32), pltpu.VMEM((heads, tokens, width), BF16)]
         + [pltpu.VMEM(square, BF16)] * 2
         + [pltpu.VMEM((heads * width, tokens), BF16),
@@ -401,7 +414,7 @@
            pltpu.VMEM((sections - 1, features, tokens), BF16)]
         + [dma((heads,))] * 4 + [dma((sections,))] * 2 + [dma((sections - 1,))] * 2,
         compiler_params=pltpu.CompilerParams(
-            collective_id=0, has_side_effects=True, vmem_limit_bytes=24 << 20),
+            collective_id=0, has_side_effects=True, vmem_limit_bytes=58 << 20),
         name="tail",
     )(m, b, r, o, y, cot, out_weight)
     return output, value_grads

time: 73.2 us -> 72.5 us (level)
  local copies, waits for them, and re-layouts: 15.2 us -> 10.1 us
  Pallas kernels: 41.4 us -> 46 us
    unnamed x24 -> x4, local copies, waits for them, and re-layouts: 13.8 us -> 8.05 us
    pallas_call x1, Pallas kernels: 26.3 us -> 28.9 us  [per_device(): pl.pallas_call(functools.partial(tail_kernel, devices, sections), in_spec...]
    pallas_call x1, Pallas kernels: 15.2 us -> 17.1 us  [per_device(): pl.pallas_call(local_kernel, grid=(groups,), in_specs=[whole(8, tokens),...]
  transfers between devices with their start and end apart: 1 -> 1, of which waited for: 0 -> 0; matrix products, arithmetic and copies ran while one was open for 7% -> 9% of each run, Pallas kernels for 21% -> 24%
where the time goes in v4:
time: 72.5 us; the launch traced here: 71.6 us
  Pallas kernels  46 us (63%)
  between operations  14 us (19%)
  local copies, waits for them, and re-layouts  10.1 us (14%)
    pallas_call x1, Pallas kernels, per_device(): pl.pallas_call(functools.partial(tail_kernel, devices, sections), in_spec...  28.9 us
    pallas_call x1, Pallas kernels, per_device(): pl.pallas_call(local_kernel, grid=(groups,), in_specs=[whole(8, tokens),...  17.1 us
    unnamed x4, local copies, waits for them, and re-layouts  8.05 us
  transfers between devices with their start and end apart: 1, of which 0 were waited for; matrix products, arithmetic and copies ran while one was open for 9% of the time, Pallas kernels for 24%

profile of v4, /device:TPU:0, one launch (start us, length us, event | category | flops | bytes accessed | tf_op | source)
XLA Modules:
  0.0 71.6 jit_solution(14137836450237410594)
XLA Ops:
  7.2 0.0 all-gather.2.cloned.1.call-start
  7.2 0.7 all-gather.2.cloned.1.call-update
  7.9 0.7 convert_element_type.3
  8.6 0.7 reshape.21
  9.3 0.7 fusion
  10.0 1.9 %copy.10 = bf16[32,8,2,512]{3,1,2,0:T(8,128)(2,1)} copy(bf16[32,8,2,512]{3,2,1,0:T(2,128)(2,1)} %bitcast.6) | data formatting | bytes 1048576
  11.9 1.9 %copy.11 = bf16[32,8,2,512]{3,1,2,0:T(8,128)(2,1)} copy(bf16[32,8,2,512]{3,2,1,0:T(2,128)(2,1)} %bitcast.7) | data formatting | bytes 1048576
  13.8 0.6 concatenate.3.rows_ref
  14.5 17.1 %local.1 = (bf16[4,384,512]{2,1,0:T(8,128)(2,1)}, bf16[4,256,128]{2,1,0:T(8,128)(2,1)}, f32[4,128,128]{2,1,0:T(8,128)}, f32[4,256,128]{2,1,0:T(8,128)}, f32[4,128,128]{2,1,0:T(8,128)}) custom-call(f32[2,8,256]{2,1,0:T(8,128)} %concatenate.3.rows_ref, bf16[256,512]{1,0:T(8,128)(2,1)} %q_ref.1, bf16[256,1024]{1,0:T(8,128)(2,1)} %bitcast.8, ...), custom_call_target="tpu_custom_call" | custom-call | flops 8589934592 | bytes 8388608 | tf_op jit(solution)/shard_map/local/pallas_call | solution.py:379
  31.6 0.0 all-gather.2.cloned.1.call-done.cot_hbm
  31.6 28.9 %tail.1 = (bf16[512,256]{1,0:T(8,128)(2,1)}, f32[256,2,512]{2,1,0:T(2,128)}) custom-call(f32[4,128,128]{2,1,0:T(8,128)} %get-tuple-element.7.m_hbm, f32[4,128,128]{2,1,0:T(8,128)} %get-tuple-element.8.b_hbm, bf16[4,256,128]{2,1,0:T(8,128)(2,1)} %get-tuple-element.9.r_hbm, f32[4,256,128]{2,1,0:T(8,128)} %get-tuple-element.10.o_hbm, ...), custom_call_target="tpu_custom_call" | custom-call | tf_op jit(solution)/shard_map/tail/pallas_call | solution.py:400
  60.5 1.7 %copy.14 = bf16[512,256]{1,0:T(8,128)(2,1)} copy(bf16[512,256]{1,0:T(8,128)(2,1)} %get-tuple-element.16) | data formatting | bytes 524288
  62.2 2.6 %copy.15 = f32[256,2,512]{2,1,0:T(2,128)} copy(f32[256,2,512]{2,1,0:T(2,128)} %get-tuple-element.17) | data formatting | bytes 2097152
  (4 shorter events, 0.0 us)
Async XLA Ops:
  7.2 24.4 %all-gather.2.cloned.1.call-start = ((), (), s32[]{:S(2)}) async-start(), calls=%async_computation | async-start | bytes 1310720 | tf_op jit(solution)/shard_map/all_gather | solution.py:357
Sparse Core Ops, SparseCore 0:
  9.6 19.4 all-gather.1
